TPU v7x, 32 devices: a whole 2x2x4 slice. The times are simulated.
32 devices in a mesh: leaf: 8 (over z, y), blk: 4 (over x, core).
Axes of the slice: x: 2, y: 2, z: 4, core: 2. Of those that a mesh axis runs over, the one named last changes fastest.
Arguments:
- leaf_net: bfloat16 [8, 64, 4096], P('leaf'), may hold values from -1.5 to 1.5
- leaf_coupling: bfloat16 [8, 4096, 4096], P('leaf', 'blk'), as said below
- index_maps: int32 [12, 32], replicated, may hold values from 0 to 35, as said below
- sep_anchor: float32 [6, 512], replicated, may hold values from 0.5 to 4
- top_net: bfloat16 [64, 32768], P(None, 'leaf'), may hold values from -1.5 to 1.5
- top_coupling: bfloat16 [32768, 2048], P('leaf', 'blk'), as said below
Outputs:
- root_update: float32 [8, 4096, 4096], P('leaf', 'blk')
- top_window: float32 [32768, 2048], P('leaf', 'blk')
Inputs may be any that keep to these rules, and one draw needn't show every extreme that they name: `index_maps`: entry i of a row sends the child's block i to block entry of the parent front: values under 512 // 128 are separator blocks, value 512 // 128 + m is block m of the parent's update matrix. Each row is one-to-one and covers every separator block. A block i that goes to the update goes to a block m with m // 2 == i // 2. Each leaf_coupling[l] is symmetric, and leaf_net[l]^T leaf_net[l] + leaf_coupling[l] is positive definite. Rows 0 to 2047 of top_coupling form a symmetric matrix, and those rows of top_net^T top_net[:, :2048] + top_coupling form a positive definite matrix.
All inputs are finite; a program needn't handle non-finite values.
Results may differ from a plain program's by a relative error of at most 0.00035.
The roundings to bfloat16 on the way count: a program that leaves them out, or rounds other values in their place, can miss the bound.
Values may be sent and summed in bfloat16 or wider, within the bound.
A program may use at most 320 MiB of HBM per device.

v0:
```python
import jax
import jax.numpy as jnp
from jax import lax
from jax.sharding import PartitionSpec as P

BS = 128
LEVELS = 2
PW = 512
NF = 2


def swapped(value, axis, distance):
    mask = 2**distance
    pairs = [(source, source ^ mask) for source in range(lax.axis_size(axis))]
    return lax.ppermute(value, axis, pairs)


def spread(value, axis, source):
    kept = jnp.where(lax.axis_index(axis) == source, value, 0).astype(value.dtype)
    return lax.psum(kept, axis)


def place_blocks(update_rows, block_map, blk_pos, block_rows, sep_blocks, upd_blocks):
    local_map = lax.dynamic_slice_in_dim(block_map, blk_pos * block_rows, block_rows, 0)
    targets = jnp.concatenate(
        [
            sep_blocks + blk_pos * block_rows + jnp.arange(block_rows, dtype=jnp.int32),
            jnp.arange(sep_blocks, dtype=jnp.int32),
        ]
    )
    matches = targets[:, None] == local_map[None, :]
    source = jnp.sum(
        jnp.where(matches, jnp.arange(block_rows, dtype=jnp.int32)[None, :], 0), axis=1
    )
    present = jnp.any(matches, axis=1)
    total_blocks = sep_blocks + upd_blocks
    col_matches = jnp.arange(total_blocks, dtype=jnp.int32)[:, None] == block_map[None, :]
    col_source = jnp.sum(
        jnp.where(col_matches, jnp.arange(upd_blocks, dtype=jnp.int32)[None, :], 0), axis=1
    )
    col_present = jnp.any(col_matches, axis=1)
    blocks = update_rows.reshape(block_rows, BS, upd_blocks, BS)
    picked_rows = jnp.take(blocks, source, axis=0)
    picked_both = jnp.take(picked_rows, col_source, axis=2)
    keep = present[:, None, None, None] & col_present[None, None, :, None]
    return jnp.where(keep, picked_both, 0.0)


def sep_part(mapped, block_rows, sep_order):
    sep_blocks = sep_order // BS
    return mapped[block_rows:, :, :sep_blocks, :].reshape(sep_order, sep_order)


def per_device(leaf_net, leaf_coupling, index_maps, sep_anchor, top_net, top_coupling):
    leaf_count = lax.axis_size("leaf")
    blk_count = lax.axis_size("blk")
    leaf_pos = lax.axis_index("leaf")
    blk_pos = lax.axis_index("blk")
    net_all = leaf_net[0]
    upd_order = net_all.shape[1]
    rows_dev = upd_order // blk_count
    sep_order = sep_anchor.shape[1]
    block_rows = rows_dev // BS
    sep_blocks = sep_order // BS
    upd_blocks = upd_order // BS
    contract_last = (((1,), (1,)), ((), ()))
    contract_first = (((0,), (0,)), ((), ()))
    my_net = lax.dynamic_slice_in_dim(net_all, blk_pos * rows_dev, rows_dev, 1)
    gram_rows = lax.dot_general(my_net, net_all, contract_first, preferred_element_type=jnp.float32)
    update_rows = gram_rows + leaf_coupling[0].astype(jnp.float32)
    node_base = 0
    parent_base = 0
    level_width = leaf_count
    for level_num in range(LEVELS):
        node_own = leaf_pos >> level_num
        map_own = lax.dynamic_index_in_dim(index_maps, node_base + node_own, 0, keepdims=False)
        map_other = lax.dynamic_index_in_dim(
            index_maps, node_base + (node_own ^ 1), 0, keepdims=False
        )
        anchor_row = lax.dynamic_index_in_dim(
            sep_anchor, parent_base + (node_own >> 1), 0, keepdims=False
        )
        mapped_own = place_blocks(update_rows, map_own, blk_pos, block_rows, sep_blocks, upd_blocks)
        other_rows = swapped(update_rows, "leaf", level_num)
        mapped_other = place_blocks(
            other_rows, map_other, blk_pos, block_rows, sep_blocks, upd_blocks
        )
        combined = mapped_own + mapped_other
        pivot_sum = lax.psum(sep_part(combined, block_rows, sep_order), "blk")
        pivot_block = pivot_sum + jnp.diag(anchor_row)
        factor = jnp.linalg.cholesky(pivot_block)
        front_rows = combined[:block_rows].reshape(rows_dev, sep_order + upd_order)
        below_rows = jax.scipy.linalg.solve_triangular(
            factor, front_rows[:, :sep_order].T, lower=True
        ).T
        below_rows = below_rows.astype(jnp.bfloat16)
        product = lax.dot_general(
            below_rows,
            lax.all_gather(below_rows, "blk", axis=0, tiled=True),
            contract_last,
            preferred_element_type=jnp.float32,
        )
        update_rows = front_rows[:, sep_order:] - product
        node_base = node_base + level_width
        parent_base = parent_base + level_width // 2
        level_width = level_width // 2
    root_update = update_rows[None]
    rows_top = top_net.shape[1]
    col_first = blk_pos * PW
    source_leaf = col_first // rows_top
    offset_rows = col_first % rows_top
    net_piece = lax.dynamic_slice_in_dim(top_net, offset_rows, PW, 1)
    column_net = spread(net_piece, "leaf", source_leaf)
    window = lax.dot_general(
        top_net, column_net, contract_first, preferred_element_type=jnp.float32
    )
    window = window + top_coupling.astype(jnp.float32)
    global_rows = leaf_pos * rows_top + jnp.arange(rows_top, dtype=jnp.int32)
    for panel_num in range(NF):
        panel_first = panel_num * PW
        owner_leaf = panel_first // rows_top
        local_first = panel_first - owner_leaf * rows_top
        diag_piece = window[local_first : local_first + PW]
        pivot_block = spread(diag_piece, "leaf", owner_leaf)
        factor = jnp.linalg.cholesky(pivot_block)

        def factor_panel(current):
            solved = jax.scipy.linalg.solve_triangular(factor, current.T, lower=True).T
            place_at = jnp.clip(panel_first - leaf_pos * rows_top, 0, rows_top - PW)
            placed = lax.dynamic_update_slice(solved, factor, (place_at, jnp.int32(0)))
            in_block = (global_rows >= panel_first) & (global_rows < panel_first + PW)
            below_block = global_rows >= panel_first + PW
            return jnp.where(
                below_block[:, None], solved, jnp.where(in_block[:, None], placed, 0.0)
            )

        def skip_panel(current):
            return jnp.zeros_like(current)

        panel_full = lax.cond(blk_pos == panel_num, factor_panel, skip_panel, window)
        rounded = panel_full.astype(jnp.bfloat16)
        panel_rows = spread(rounded, "blk", panel_num)
        column_rows = spread(
            lax.dynamic_slice_in_dim(panel_rows, offset_rows, PW, 0), "leaf", source_leaf
        )
        trailing = window - lax.dot_general(
            panel_rows, column_rows, contract_last, preferred_element_type=jnp.float32
        )
        window = jnp.where(blk_pos == panel_num, panel_full, trailing)
    return (root_update, window)


def solution(mesh):
    return jax.shard_map(
        per_device,
        mesh=mesh,
        in_specs=(
            P("leaf", None, None),
            P("leaf", "blk", None),
            P(),
            P(),
            P(None, "leaf"),
            P("leaf", "blk"),
        ),
        out_specs=(P("leaf", "blk", None), P("leaf", "blk")),
        check_vma=False,
    )
```

profile of v0, /device:TPU:0, one launch (start us, length us, event | category | flops | bytes accessed | tf_op | source)
XLA Modules:
  0.0 2051.7 jit_solution(16685942397402395372)
XLA Ops:
  9.0 11.9 convert_add_fusion
  23.9 14.2 copy.94
  39.6 16.3 gather_fusion
  66.0 16.6 copy.68
  82.9 24.1 %gather_fusion.1 = f32[36,12,128,128]{3,2,1,0:T(8,128)} fusion(f32[12,128,32,128]{3,1,2,0:T(8,128)} %copy.68, s32[1024]{0:T(1024)S(1)} %pad_clamp_fusion.6), kind=kCustom, calls=%fused_computation.1.clone | custom fusion | bytes 56623248 | tf_op jit(solution)/shard_map/jit(_take)/gather | solution.py:44
  109.1 275.3 %collective-permute-done = f32[1024,4096]{1,0:T(8,128)} collective-permute-done((f32[1024,4096]{1,0:T(8,128)}, f32[1024,4096]{1,0:T(8,128)}, u32[]{:S(2)}, u32[]{:S(2)}) %collective-permute-start) | collective-permute-done | bytes 16777248 | tf_op jit(solution)/shard_map/ppermute | solution.py:15
  384.5 14.2 copy.95
  398.6 16.4 gather_fusion.2
  425.2 17.0 copy.69
  442.2 24.0 %gather_fusion.3 = f32[36,12,128,128]{3,2,1,0:T(8,128)} fusion(f32[12,128,32,128]{3,1,2,0:T(8,128)} %copy.69, s32[1024]{0:T(1024)S(1)} %pad_clamp_fusion.4), kind=kCustom, calls=%fused_computation.5.clone | custom fusion | bytes 56623248 | tf_op jit(solution)/shard_map/jit(_take)/gather | solution.py:44
  466.2 27.5 %fusion.47 = f32[12,128,36,128]{3,1,0,2:T(8,128)} fusion(f32[36,12,128,128]{3,2,1,0:T(8,128)} %gather_fusion.3, f32[36,12,128,128]{3,2,1,0:T(8,128)} %gather_fusion.1, pred[36]{0:T(512)(128)(4,1)S(1)} %get-tuple-element.433, pred[36]{0:T(512)(128)(4,1)S(1)} %get-tuple-element.434, pred[12,36]{0,1:T(8,128)(4,1)S(1)} %broadcast_and_fusion.1, ...), kind=kLoop, calls=%fused_computation.104 | loop fusion | flops 35389440 | bytes 84935592 | tf_op jit(solution)/shard_map/add | solution.py:88
  497.8 13.0 slice.184
  510.8 18.8 copy.70
  555.4 11.7 cholesky.462
  581.2 11.7 cholesky.481
  630.3 12.1 cholesky.519
  662.1 39.3 %custom-call.42 = f32[4,128,128]{1,2,0:T(8,128)S(1)} custom-call(f32[4,128,128]{2,1,0:T(8,128)S(1)} %get-tuple-element.73), custom_call_target="InvertDiagBlocksLowerTriangular" | custom-call | tf_op jit(solution)/shard_map/jit(_solve_triangular)/triangular_solve | solution.py:93
  710.5 12.1 slice.185
  722.6 17.5 copy.92
  746.6 13.1 convolution_subtract_fusion.4
  768.2 62.5 %all-reduce.15.cloned.1.call-done = bf16[64,512]{1,0:T(8,128)(2,1)} async-done(((bf16[64,512]{1,0:T(8,128)(2,1)}), bf16[64,512]{1,0:T(8,128)(2,1)}) %all-reduce.15.cloned.1.call-update) | async-done | bytes 65552 | tf_op jit(solution)/shard_map/psum | solution.py:20
  839.2 96.7 %all-reduce.17.cloned.1.call-done = f32[512,512]{0,1:T(8,128)} async-done(((f32[512,512]{0,1:T(8,128)}), f32[512,512]{0,1:T(8,128)}) %all-reduce.17.cloned.1.call-update) | async-done | bytes 1048592 | tf_op jit(solution)/shard_map/psum | solution.py:20
  1019.6 108.6 %conditional.2 = (f32[4096,512]{0,1:T(8,128)}, bf16[4096,512]{0,1:T(8,128)(2,1)}) conditional(s32[]{:T(128)} %convert_element_type.57, () %tuple.34, (s32[4096]{0:T(1024)S(1)}, f32[4096,512]{0,1:T(8,128)}, pred[512,512]{1,0:T(8,128)(4,1)S(1)}, s32[]{:T(128)}, pred[128,128]{1,0:T(8,128)(4,1)S(1)}, /*index=5*/f32[512,512]{1,0:T(8,128)S(1)}, ...), branch_computations={%region_28.33_spmd, %region_29.35_spmd.clone} | conditional | flops 8078901760 | bytes 124293560 | solution.py:140
  1030.3 11.9 while.10
  1042.3 39.5 %custom-call.53 = f32[4,128,128]{1,2,0:T(8,128)S(1)} custom-call(f32[4,128,128]{2,1,0:T(8,128)S(1)} %get-tuple-element.213), custom_call_target="InvertDiagBlocksLowerTriangular" | custom-call | tf_op jit(solution)/shard_map/cond/branch_1_fun/jit(_solve_triangular)/triangular_solve | solution.py:128
  1132.9 87.1 %all-reduce.19.cloned.1.call-done = bf16[4096,512]{0,1:T(8,128)(2,1)} async-done(((bf16[4096,512]{0,1:T(8,128)(2,1)}), bf16[4096,512]{0,1:T(8,128)(2,1)}) %all-reduce.19.cloned.1.call-update) | async-done | bytes 4194320 | tf_op jit(solution)/shard_map/psum | solution.py:20
  1222.7 71.6 %all-reduce.21.cloned.1.call-done = bf16[512,512]{0,1:T(8,128)(2,1)} async-done(((bf16[512,512]{0,1:T(8,128)(2,1)}), bf16[512,512]{0,1:T(8,128)(2,1)}) %all-reduce.21.cloned.1.call-update) | async-done | bytes 524304 | tf_op jit(solution)/shard_map/psum | solution.py:20
  1311.7 73.6 %all-reduce.23.cloned.1.call-done = f32[512,512]{0,1:T(8,128)} async-done(((f32[512,512]{0,1:T(8,128)}), f32[512,512]{0,1:T(8,128)}) %all-reduce.23.cloned.1.call-update) | async-done | bytes 1048592 | tf_op jit(solution)/shard_map/psum | solution.py:20
  1465.7 11.7 cholesky.735
  1477.4 16.8 conditional.3
  1496.7 14.1 copy.98
  1510.8 16.3 gather_fusion.4
  1537.2 16.6 copy.74
  1553.8 24.1 %gather_fusion.5 = f32[36,12,128,128]{3,2,1,0:T(8,128)} fusion(f32[12,128,32,128]{3,1,2,0:T(8,128)} %copy.74, s32[1024]{0:T(1024)S(1)} %pad_clamp_fusion.2), kind=kCustom, calls=%fused_computation.6.clone | custom fusion | bytes 56623248 | tf_op jit(solution)/shard_map/jit(_take)/gather | solution.py:44
  1577.9 14.2 copy.99
  1592.1 16.9 gather_fusion.6
  1619.2 17.0 copy.75
  1636.3 24.8 %gather_fusion.7 = f32[36,12,128,128]{3,2,1,0:T(8,128)} fusion(f32[12,128,32,128]{3,1,2,0:T(8,128)} %copy.75, s32[1024]{0:T(1024)} %pad_clamp_fusion), kind=kCustom, calls=%fused_computation.7.clone | custom fusion | bytes 56623248 | tf_op jit(solution)/shard_map/jit(_take)/gather | solution.py:44
  1661.1 27.6 %fusion.46 = f32[12,128,36,128]{3,1,0,2:T(8,128)} fusion(f32[36,12,128,128]{3,2,1,0:T(8,128)} %gather_fusion.7, f32[36,12,128,128]{3,2,1,0:T(8,128)} %gather_fusion.5, pred[36]{0:T(512)(128)(4,1)S(1)} %copy-done.41, pred[36]{0:T(512)(128)(4,1)S(1)} %copy-done.42, pred[12,36]{0,1:T(8,128)(4,1)S(1)} %copy-done.25, pred[12,36]{0,1:T(8,128)(4,1)S(1)} %copy-done.26), kind=kLoop, calls=%fused_computation.101 | loop fusion | flops 35389440 | bytes 84935592 | tf_op jit(solution)/shard_map/add | solution.py:88
  1693.5 12.9 slice.188
  1706.4 18.7 copy.76
  1742.5 75.4 %all-reduce.13.cloned.1.call-done = f32[512,512]{0,1:T(8,128)} async-done(((f32[512,512]{0,1:T(8,128)}), f32[512,512]{0,1:T(8,128)}) %all-reduce.13.cloned.1.call-update) | async-done | bytes 1048592 | tf_op jit(solution)/shard_map/psum | solution.py:89
  1825.5 11.7 cholesky.534
  1900.5 11.9 cholesky.591
  1931.6 39.3 %custom-call.46 = f32[4,128,128]{1,2,0:T(8,128)S(1)} custom-call(f32[4,128,128]{2,1,0:T(8,128)S(1)} %get-tuple-element.74), custom_call_target="InvertDiagBlocksLowerTriangular" | custom-call | tf_op jit(solution)/shard_map/jit(_solve_triangular)/triangular_solve | solution.py:93
  2000.1 12.4 slice.189
  2012.5 17.5 copy.93
  2030.7 13.2 subtract_bitcast_fusion
  (356 shorter events, 604.7 us)
Async XLA Ops:
  8.0 1.1 copy-start
  8.0 539.0 %all-reduce.11.cloned.1.call-start = ((), (), s32[]{:S(2)}) async-start(), calls=%async_computation | async-start | bytes 2097152 | tf_op jit(solution)/shard_map/psum | solution.py:89
  21.0 363.5 %collective-permute-start = (f32[1024,4096]{1,0:T(8,128)}, f32[1024,4096]{1,0:T(8,128)}, u32[]{:S(2)}, u32[]{:S(2)}) collective-permute-start(f32[1024,4096]{1,0:T(8,128)} %convert_add_fusion), channel_id=1, source_target_pairs={{0,4},{4,0},{8,12},{12,8},{16,20},{20,16},{24,28},{28,24},{1,5},{5... | collective-permute-start | bytes 50331656 | tf_op jit(solution)/shard_map/ppermute | solution.py:15
  23.9 14.3 copy-start.32
  82.7 24.4 %copy-start.39 = (s32[32]{0:T(128)}, s32[32]{0:T(128)S(1)}, u32[]{:S(2)}) copy-start(s32[32]{0:T(128)S(1)} %get-tuple-element.410) | copy-start | bytes 388
  82.7 25.0 %copy-start.37 = (s32[32]{0:T(128)}, s32[32]{0:T(128)S(1)}, u32[]{:S(2)}) copy-start(s32[32]{0:T(128)S(1)} %get-tuple-element.407) | copy-start | bytes 388
  496.4 250.1 %all-gather.3.cloned.1.call-start = ((), (), s32[]{:S(2)}) async-start(), calls=%async_computation.1 | async-start | bytes 5242880 | tf_op jit(solution)/shard_map/all_gather | solution.py:99
  540.4 6.5 copy-start.5
  547.0 157.1 %copy-start.17 = (f32[512,1024]{1,0:T(8,128)}, f32[512,1024]{1,0:T(8,128)S(1)}, u32[]{:S(2)}) copy-start(f32[512,1024]{1,0:T(8,128)S(1)} %slice_bitcast_fusion.17) | copy-start | bytes 6291460
  710.5 120.3 %all-reduce.15.cloned.1.call-start = ((), (), s32[]{:S(2)}) async-start(), calls=%async_computation.4 | async-start | bytes 131072 | tf_op jit(solution)/shard_map/psum | solution.py:20
  740.1 21.1 %copy-start.22 = (bf16[64,4096]{1,0:T(8,128)(2,1)S(1)}, bf16[64,4096]{1,0:T(8,128)(2,1)}, u32[]{:S(2)}) copy-start(bf16[64,4096]{1,0:T(8,128)(2,1)} %param.23) | copy-start | bytes 1572868
  759.7 818.2 %collective-permute-start.1 = (f32[1024,4096]{1,0:T(8,128)}, f32[1024,4096]{1,0:T(8,128)}, u32[]{:S(2)}, u32[]{:S(2)}) collective-permute-start(f32[1024,4096]{1,0:T(8,128)} %convolution_subtract_fusion.4), channel_id=1, source_target_pairs={{0,8},{4,12},{8,0},{12,4},{16,24},{20,28},{24,16},{28,20},{1,9},{5... | collective-permute-start | bytes 50331656 | tf_op jit(solution)/shard_map/ppermute | solution.py:15
  761.9 174.0 %all-reduce.17.cloned.1.call-start = ((), (), s32[]{:S(2)}) async-start(), calls=%async_computation.5 | async-start | bytes 2097152 | tf_op jit(solution)/shard_map/psum | solution.py:20
  834.3 3.4 copy-start.3
  838.8 381.1 %all-reduce.19.cloned.1.call-start = ((), (), s32[]{:S(2)}) async-start(), calls=%async_computation.6 | async-start | bytes 8388608 | tf_op jit(solution)/shard_map/psum | solution.py:20
  1005.4 1.0 copy-start.18
  1018.4 1.2 copy-start.14
  1090.8 15.3 copy-start.7
  1097.6 8.5 copy-start.9
  1106.1 3.9 copy-start.11
  1128.2 4.5 copy-start.40
  1128.2 4.6 copy-start.33
  1128.2 93.8 %copy-start.38 = (s32[32]{0:T(128)S(1)}, s32[32]{0:T(128)}, u32[]{:S(2)}) copy-start(s32[32]{0:T(128)} %copy-done.37) | copy-start | bytes 388
  1132.7 161.6 %all-reduce.21.cloned.1.call-start = ((), (), s32[]{:S(2)}) async-start(), calls=%async_computation.7 | async-start | bytes 1048576 | tf_op jit(solution)/shard_map/psum | solution.py:20
  1221.9 163.4 %all-reduce.23.cloned.1.call-start = ((), (), s32[]{:S(2)}) async-start(), calls=%async_computation.8 | async-start | bytes 2097152 | tf_op jit(solution)/shard_map/psum | solution.py:20
  1294.3 15.4 copy-start.34
  1294.3 15.4 copy-start.29
  1294.3 16.0 copy-start.31
  1294.3 16.0 copy-start.35
  1294.3 16.7 copy-start.30
  1294.3 16.7 copy-start.36
  1304.6 3.4 copy-start.2
  1308.0 169.3 %copy-start.13 = (f32[512,512]{1,0:T(8,128)S(1)}, f32[512,512]{1,0:T(8,128)}, u32[]{:S(2)}) copy-start(f32[512,512]{1,0:T(8,128)} %copy-done.12) | copy-start | bytes 3145732
  1308.0 169.4 %copy-start.15 = (f32[512,512]{1,0:T(8,128)S(1)}, f32[512,512]{1,0:T(8,128)}, u32[]{:S(2)}) copy-start(f32[512,512]{1,0:T(8,128)} %copy-done.14) | copy-start | bytes 3145732
  1309.1 382.3 %all-reduce.25.cloned.1.call-start = ((), (), s32[]{:S(2)}) async-start(), calls=%async_computation.9 | async-start | bytes 8388608 | tf_op jit(solution)/shard_map/psum | solution.py:20
  1389.6 1.0 copy-start.19
  1496.6 321.2 %all-reduce.13.cloned.1.call-start = ((), (), s32[]{:S(2)}) async-start(), calls=%async_computation.2 | async-start | bytes 2097152 | tf_op jit(solution)/shard_map/psum | solution.py:89
  1636.3 24.8 %copy-start.25 = (pred[12,36]{0,1:T(8,128)(4,1)S(1)}, pred[12,36]{0,1:T(8,128)(4,1)}, u32[]{:S(2)}) copy-start(pred[12,36]{0,1:T(8,128)(4,1)} %broadcast_and_fusion) | copy-start | bytes 1300
  1636.3 24.8 %copy-start.26 = (pred[12,36]{0,1:T(8,128)(4,1)S(1)}, pred[12,36]{0,1:T(8,128)(4,1)}, u32[]{:S(2)}) copy-start(pred[12,36]{0,1:T(8,128)(4,1)} %broadcast_and_fusion.3) | copy-start | bytes 1300
  1636.3 24.8 %copy-start.41 = (pred[36]{0:T(512)(128)(4,1)S(1)}, pred[36]{0:T(512)(128)(4,1)}, u32[]{:S(2)}) copy-start(pred[36]{0:T(512)(128)(4,1)} %get-tuple-element.429) | copy-start | bytes 112
  1636.3 24.8 %copy-start.42 = (pred[36]{0:T(512)(128)(4,1)S(1)}, pred[36]{0:T(512)(128)(4,1)}, u32[]{:S(2)}) copy-start(pred[36]{0:T(512)(128)(4,1)} %get-tuple-element.430) | copy-start | bytes 112
  1691.4 288.9 %all-reduce.27.cloned.1.call-start = ((), (), s32[]{:S(2)}) async-start(), calls=%async_computation.10 | async-start | bytes 1048576 | tf_op jit(solution)/shard_map/psum | solution.py:20
  1693.5 337.2 %all-gather.5.cloned.1.call-start = ((), (), s32[]{:S(2)}) async-start(), calls=%async_computation.3 | async-start | bytes 5242880 | tf_op jit(solution)/shard_map/all_gather | solution.py:99
  1725.1 92.7 %copy-start.27 = (f32[1,512]{1,0:T(1,128)S(1)}, f32[1,512]{1,0:T(1,128)}, u32[]{:S(2)}) copy-start(f32[1,512]{1,0:T(1,128)} %get-tuple-element.405) | copy-start | bytes 6148
  1735.8 6.5 copy-start.4
  1742.5 229.1 %copy-start.16 = (f32[512,1024]{1,0:T(8,128)}, f32[512,1024]{1,0:T(8,128)S(1)}, u32[]{:S(2)}) copy-start(f32[512,1024]{1,0:T(8,128)S(1)} %slice_bitcast_fusion.16) | copy-start | bytes 6291460
  1820.2 100.2 %copy-start.24 = (s32[4,2]{0,1:T(2,128)S(1)}, s32[4,2]{0,1:T(2,128)}, u32[]{:S(2)}) copy-start(s32[4,2]{0,1:T(2,128)} %copy-done.23) | copy-start | bytes 100
  2030.7 13.2 copy-start.1
  (5 other events, 4.1 us)
Sparse Core Ops, SparseCore 0:
  496.6 37.5 all-reduce.10
  710.6 35.9 all-gather.2
  1132.8 87.1 all-reduce.18
  1496.7 175.8 all-reduce.24
  1691.5 126.2 all-reduce.12
  1821.5 73.3 all-reduce.26
  1980.4 50.2 all-gather.4
Sparse Core Ops, SparseCore 1:
  761.9 68.8 all-reduce.14
  838.9 96.9 all-reduce.16
  1222.0 72.2 all-reduce.20
  1309.2 76.0 all-reduce.22
where the time goes:
time: 2080 us; the launch traced here: 2050 us
  waiting for transfers between devices  750 us (36%)
  other arithmetic  589 us (28%)
  local copies, waits for them, and re-layouts  544 us (26%)
  matrix products  128 us (6%)
  between operations  21.8 us (1%)
    psum x7, waiting for transfers between devices, spread(): return lax.psum(kept, axis)  392 us
    another operation x57, other arithmetic, per_device(): factor = jnp.linalg.cholesky(pivot_block)  320 us
    ppermute x2, waiting for transfers between devices, swapped(): return lax.ppermute(value, axis, pairs)  275 us
    unnamed x86, local copies, waits for them, and re-layouts  157 us
    gather x4, local copies, waits for them, and re-layouts, place_blocks(): picked_both = jnp.take(picked_rows, col_source, axis=2)  96.9 us
    another operation x6, other arithmetic, per_device(): jax.scipy.linalg.solve_triangular(factor, front_rows[:, :sep_order].T, lo...  83.4 us
    psum x2, waiting for transfers between devices, per_device(): pivot_sum = lax.psum(sep_part(combined, block_rows, sep_order), 'blk')  75.4 us
    select_n x4, local copies, waits for them, and re-layouts, place_blocks(): picked_rows = jnp.take(blocks, source, axis=0)  67.3 us
  transfers between devices with their start and end apart: 13, of which 9 were waited for; matrix products, arithmetic and copies ran while one was open for 45% of the time, Pallas kernels for 0%

commit v1 on v0

v1 whole, which is shorter than its diff:
```python
import jax
import jax.numpy as jnp
from jax import lax
from jax.experimental import pallas as pl
from jax.experimental.pallas import tpu as pltpu
from jax.sharding import PartitionSpec as P

BS = 128
LEVELS = 2
PW = 512
GROUP = 2
LAST = (((1,), (1,)), ((), ()))
FIRST = (((0,), (0,)), ((), ()))
HIGH = lax.Precision.HIGHEST


def gram(left, right):
    return lax.dot_general(left, right, FIRST, preferred_element_type=jnp.float32)


def outer(left, right):
    return lax.dot_general(left, right, LAST, preferred_element_type=jnp.float32)


def solved(rows, inverse):
    return lax.dot_general(rows, inverse, LAST, precision=HIGH, preferred_element_type=jnp.float32)


def factor_inverse(block):
    factor = jnp.linalg.cholesky(block)
    identity = jnp.eye(block.shape[0], dtype=jnp.float32)
    return factor, jax.scipy.linalg.solve_triangular(factor, identity, lower=True)


def swapped(value, axis, mask):
    return lax.ppermute(value, axis, [(s, s ^ mask) for s in range(lax.axis_size(axis))])


def total(value, axis):
    mask = 1
    while mask < lax.axis_size(axis):
        value = value + swapped(value, axis, mask)
        mask *= 2
    return value


def leaf_spread(value, source_of):
    leaf_count, blk_count = lax.axis_size("leaf"), lax.axis_size("blk")
    blk_pos = lax.axis_index("blk")
    sources = jnp.array([source_of(b) for b in range(blk_count)], jnp.int32)
    rank = lax.axis_index("leaf") ^ sources[blk_pos]
    step = leaf_count // 2
    while step:
        pairs = []
        for b in range(blk_count):
            for r in range(0, leaf_count, 2 * step):
                src = source_of(b)
                pairs.append(((r ^ src) * blk_count + b, ((r + step) ^ src) * blk_count + b))
        got = lax.ppermute(value, ("leaf", "blk"), pairs)
        value = jnp.where(rank % (2 * step) == step, got, value)
        step //= 2
    return value


def first_two(value):
    blk_count = lax.axis_size("blk")
    blk_pos = lax.axis_index("blk")
    step = 2
    while step < blk_count:
        got = lax.ppermute(value, "blk", [(s, s + step) for s in range(step)])
        value = jnp.where((blk_pos >= step) & (blk_pos < 2 * step), got, value)
        step *= 2
    mate = swapped(value, "blk", 1)
    even = blk_pos % 2 == 0
    return jnp.where(even, value, mate), jnp.where(even, mate, value)


def merge_kernel(scal, own, oth, lrow, lall, out):
    blocks = own.shape[1] // BS
    first = scal[1] + GROUP * (scal[0] + pl.program_id(0))
    step = 4
    for quarter in range(blocks // step):
        width = step * BS
        prod = outer(lrow[...], lall[quarter * width : (quarter + 1) * width, :])
        for half in range(GROUP):
            row_a = scal[2 + first + half]
            row_b = scal[2 + blocks + first + half]
            at_a = pl.multiple_of((jnp.maximum(row_a, 0) % GROUP) * BS, BS)
            at_b = pl.multiple_of((jnp.maximum(row_b, 0) % GROUP) * BS, BS)
            for c in range(step):
                col = quarter * step + c
                col_a = scal[2 + col]
                col_b = scal[2 + blocks + col]
                ca = pl.multiple_of(jnp.maximum(col_a, 0) * BS, BS)
                cb = pl.multiple_of(jnp.maximum(col_b, 0) * BS, BS)
                a = own[pl.ds(at_a, BS), pl.ds(ca, BS)]
                b = oth[pl.ds(at_b, BS), pl.ds(cb, BS)]
                a = jnp.where((row_a >= 0) & (col_a >= 0), a, 0.0)
                b = jnp.where((row_b >= 0) & (col_b >= 0), b, 0.0)
                piece = prod[half * BS : (half + 1) * BS, c * BS : (c + 1) * BS]
                out[half * BS : (half + 1) * BS, col * BS : (col + 1) * BS] = a + b - piece


def merge(group_first, block_first, src_own, src_oth, own, oth, lrow, lall):
    rows, cols = oth.shape
    sep = lrow.shape[1]
    tall = GROUP * BS
    scal = jnp.concatenate(
        [jnp.stack([jnp.int32(group_first), jnp.int32(block_first)]), src_own, src_oth]
    )
    spec = pltpu.PrefetchScalarGridSpec(
        num_scalar_prefetch=1,
        grid=(rows // tall,),
        in_specs=[
            pl.BlockSpec((tall, cols), lambda i, s: (s[0] + i, 0)),
            pl.BlockSpec((tall, cols), lambda i, s: (i, 0)),
            pl.BlockSpec((tall, sep), lambda i, s: (s[0] + i, 0)),
            pl.BlockSpec((cols, sep), lambda i, s: (0, 0)),
        ],
        out_specs=pl.BlockSpec((tall, cols), lambda i, s: (s[0] + i, 0)),
    )
    return pl.pallas_call(
        merge_kernel,
        out_shape=jax.ShapeDtypeStruct(own.shape, jnp.float32),
        grid_spec=spec,
        input_output_aliases={1: 0},
        compiler_params=pltpu.CompilerParams(vmem_limit_bytes=48 * 2**20),
        cost_estimate=pl.CostEstimate(
            flops=2 * rows * cols * sep,
            bytes_accessed=12 * rows * cols + 2 * sep * cols,
            transcendentals=0,
        ),
    )(scal, own, oth, lrow, lall)


def sources(block_map, first, count):
    targets = first + jnp.arange(count, dtype=jnp.int32)
    match = targets[:, None] == block_map[None, :]
    ids = jnp.arange(block_map.shape[0], dtype=jnp.int32)[None, :]
    return jnp.max(jnp.where(match, ids, -1), axis=1)


def take_columns(rows, src):
    return jnp.concatenate(
        [lax.dynamic_slice_in_dim(rows, src[k] * BS, BS, 1) for k in range(src.shape[0])], axis=1
    )


def take_rows(rows, picks, keeps):
    parts = [
        jnp.where(keeps[k], lax.dynamic_slice_in_dim(rows, picks[k] * BS, BS, 0), 0.0)
        for k in range(picks.shape[0])
    ]
    return jnp.concatenate(parts, axis=0)


def front_columns(cols, upd_src, sep_src, block_first, block_rows):
    local = lax.dynamic_slice_in_dim(upd_src, block_first, block_rows, 0)
    below = take_rows(cols, jnp.maximum(local - block_first, 0), local >= 0)
    here = (sep_src >= block_first) & (sep_src < block_first + block_rows)
    pivot = take_rows(cols, jnp.where(here, sep_src - block_first, 0), here)
    return below, pivot


def top_part(top_net, top_coupling):
    leaf_pos, blk_pos = lax.axis_index("leaf"), lax.axis_index("blk")
    rows_top = top_net.shape[1]
    lead = 2 * PW
    coup0, coup1 = first_two(top_coupling)
    piece = lax.dynamic_slice_in_dim(top_net, (blk_pos * PW) % rows_top, PW, 1)
    net_mine = leaf_spread(piece, lambda b: (b * PW) // rows_top)
    lead_mine = leaf_spread(top_coupling[:lead], lambda b: 0)
    both0, both1 = first_two(jnp.concatenate([lead_mine, net_mine], axis=0))
    lead0, net0 = both0[:lead].astype(jnp.float32), both0[lead:]
    lead1, net1 = both1[:lead].astype(jnp.float32), both1[lead:]
    mine = lead_mine.astype(jnp.float32)
    factor0, inv0 = factor_inverse(gram(net0, net0) + lead0[:PW])
    cross = solved(gram(net1, net0) + lead0[PW:], inv0).astype(jnp.bfloat16)
    factor1, inv1 = factor_inverse(gram(net1, net1) + lead1[PW:] - outer(cross, cross))
    q0 = solved((gram(net0, net_mine) + mine[:PW]).T, inv0).astype(jnp.bfloat16)
    q1 = solved((gram(net1, net_mine) + mine[PW:]).T - outer(q0, cross), inv1)
    q1 = q1.astype(jnp.bfloat16)
    holds = leaf_pos == 0
    row = (leaf_pos * rows_top + jnp.arange(rows_top, dtype=jnp.int32))[:, None]

    def panel(current, inverse, factor, first):
        full = solved(current, inverse)
        placed = lax.dynamic_update_slice(full, factor, (first, 0))
        full = jnp.where(holds, placed, full)
        return jnp.where(row >= first, full, 0.0)

    p0 = panel(gram(top_net, net0) + coup0.astype(jnp.float32), inv0, factor0, 0)
    b0 = p0.astype(jnp.bfloat16)
    p1 = panel(
        gram(top_net, net1) + coup1.astype(jnp.float32) - outer(b0, cross), inv1, factor1, PW
    )
    b1 = p1.astype(jnp.bfloat16)
    rest = gram(top_net, net_mine) + top_coupling.astype(jnp.float32)
    rest = rest - outer(b0, q0) - outer(b1, q1)
    return jnp.where(blk_pos == 0, p0, jnp.where(blk_pos == 1, p1, rest))


def per_device(leaf_net, leaf_coupling, index_maps, sep_anchor, top_net, top_coupling):
    leaf_count = lax.axis_size("leaf")
    leaf_pos, blk_pos = lax.axis_index("leaf"), lax.axis_index("blk")
    net_own = leaf_net[0]
    coup_own = leaf_coupling[0]
    rows_dev, upd_order = coup_own.shape
    sep_order = sep_anchor.shape[1]
    block_rows = rows_dev // BS
    sep_blocks, upd_blocks = sep_order // BS, upd_order // BS
    block_first = blk_pos * block_rows
    groups = block_rows // GROUP

    def my_part(net):
        return lax.dynamic_slice_in_dim(net, blk_pos * rows_dev, rows_dev, 1)

    def maps(base, node):
        row = lax.dynamic_index_in_dim(index_maps, base + node, 0, keepdims=False)
        return sources(row, 0, sep_blocks), sources(row, sep_blocks, upd_blocks)

    def factor_columns(cols_own, cols_oth, own, oth, anchor):
        below_a, pivot_a = front_columns(cols_own, own[1], own[0], block_first, block_rows)
        below_b, pivot_b = front_columns(cols_oth, oth[1], oth[0], block_first, block_rows)
        pivot = total(pivot_a + pivot_b, "blk") + jnp.diag(anchor)
        inverse = factor_inverse(pivot)[1]
        lrow = solved(below_a + below_b, inverse).astype(jnp.bfloat16)
        return lrow, lax.all_gather(lrow, "blk", axis=0, tiled=True)

    own, oth = maps(0, leaf_pos), maps(0, leaf_pos ^ 1)
    net_oth = swapped(net_own, "leaf", 1)
    coup_cols = take_columns(coup_own, own[0])
    coup_cols_oth = swapped(coup_cols, "leaf", 1)
    coup_oth = swapped(coup_own, "leaf", 1)
    cols_own = gram(my_part(net_own), take_columns(net_own, own[0])) + coup_cols.astype(jnp.float32)
    cols_oth = gram(my_part(net_oth), take_columns(net_oth, oth[0])) + coup_cols_oth.astype(
        jnp.float32
    )
    lrow, lall = factor_columns(cols_own, cols_oth, own, oth, sep_anchor[leaf_pos >> 1])
    u_own = gram(my_part(net_own), net_own) + coup_own.astype(jnp.float32)
    u_oth = gram(my_part(net_oth), net_oth) + coup_oth.astype(jnp.float32)
    update = merge(0, block_first, own[1], oth[1], u_own, u_oth, lrow, lall)

    node = leaf_pos >> 1
    own, oth = maps(leaf_count, node), maps(leaf_count, node ^ 1)
    cols_own = take_columns(update, own[0])
    cols_oth = swapped(cols_own, "leaf", 2)
    tall = GROUP * BS
    pieces = []
    if groups % 2 == 0:
        side = leaf_pos & 1
        half = groups // 2
        direct = []
        for k in range(half):
            at = side * half + k
            piece = lax.dynamic_slice_in_dim(update, at * tall, tall, 0)
            direct.append((at, swapped(piece, "leaf", 2)))
        pieces = direct + [
            ((1 - side) * half + k, swapped(direct[k][1], "leaf", 1)) for k in range(half)
        ]
    else:
        pieces = [(0, swapped(update, "leaf", 2))]
    anchor = sep_anchor[leaf_count // 2 + (node >> 1)]
    lrow, lall = factor_columns(cols_own, cols_oth, own, oth, anchor)
    window = top_part(top_net, top_coupling)
    for at, piece in pieces:
        update = merge(at, block_first, own[1], oth[1], update, piece, lrow, lall)
    return (update[None], window)


def solution(mesh):
    return jax.shard_map(
        per_device,
        mesh=mesh,
        in_specs=(
            P("leaf", None, None),
            P("leaf", "blk", None),
            P(),
            P(),
            P(None, "leaf"),
            P("leaf", "blk"),
        ),
        out_specs=(P("leaf", "blk", None), P("leaf", "blk")),
        check_vma=False,
    )
```

time: 2080 us -> 1380 us (0.66)
  waiting for transfers between devices: 750 us -> 275 us
  local copies, waits for them, and re-layouts: 544 us -> 127 us
  matrix products: 128 us -> 224 us
  Pallas kernels: 0 us -> 56.6 us
  starting transfers between devices: 5.55 us -> 48.7 us
  between operations: 21.8 us -> 63.3 us
    psum x9 -> x0, waiting for transfers between devices: 467 us -> none  [the longest x7 392 us: spread(): return lax.psum(kept, axis)]
    gather x8 -> x0, local copies, waits for them, and re-layouts: 163 us -> none  [the longest x4 96.9 us: place_blocks(): picked_both = jnp.take(picked_rows, col_source, axis=2)]
    unnamed x86 -> x154, local copies, waits for them, and re-layouts: 157 us -> 26.8 us
    dot_general x6 -> x24, matrix products: 62.9 us -> 161 us  [the longest x7 86.3 us: solved(): lax.dot_general(rows, inverse, LAST, precision=HIGH, preferred_element_ty...]
    slice x10 -> x20, local copies, waits for them, and re-layouts: 91.3 us -> 14.8 us  [the longest x8 5.35 us: take_rows(): keeps[k]]
    select_n x4 -> x1, local copies, waits for them, and re-layouts: 67.3 us -> 2.35 us  [first_two(): value = jnp.where((blk_pos >= step) & (blk_pos < 2 * step), got, value)]
    add x6 -> x7, other arithmetic: 60.4 us -> 3.24 us  [the longest x4 1.68 us: factor_columns(): pivot = total(pivot_a + pivot_b, 'blk') + jnp.diag(anchor)]
    pallas_call x0 -> x5, Pallas kernels: none -> 56.6 us  [merge(): pl.pallas_call(merge_kernel, out_shape=jax.ShapeDtypeStruct(own.shape, jn...]
  transfers between devices with their start and end apart: 13 -> 24, of which waited for: 9 -> 10; matrix products, arithmetic and copies ran while one was open for 45% -> 67% of each run, Pallas kernels for 0% -> 3%
where the time goes in v1:
time: 1380 us; the launch traced here: 1370 us
  other arithmetic  574 us (42%)
  waiting for transfers between devices  275 us (20%)
  matrix products  224 us (16%)
  local copies, waits for them, and re-layouts  127 us (9%)
  between operations  63.3 us (5%)
  Pallas kernels  56.6 us (4%)
  starting transfers between devices  48.7 us (4%)
    another operation x59, other arithmetic, factor_inverse(): factor = jnp.linalg.cholesky(block)  334 us
    ppermute x14, waiting for transfers between devices, swapped(): lax.ppermute(value, axis, [(s, s ^ mask) for s in range(lax.axis_size(axi...  264 us
    another operation x9, other arithmetic, factor_inverse(): jax.scipy.linalg.solve_triangular(factor, identity, lower=True)  166 us
    dot_general x7, matrix products, solved(): lax.dot_general(rows, inverse, LAST, precision=HIGH, preferred_element_ty...  86.3 us
    dot_general x12, matrix products, gram(): lax.dot_general(left, right, FIRST, preferred_element_type=jnp.float32)  57.3 us
    pallas_call x5, Pallas kernels, merge(): pl.pallas_call(merge_kernel, out_shape=jax.ShapeDtypeStruct(own.shape, jn...  56.6 us
    another operation x53, local copies, waits for them, and re-layouts, factor_inverse(): jax.scipy.linalg.solve_triangular(factor, identity, lower=True)  51.9 us
    another operation x28, matrix products, factor_inverse(): jax.scipy.linalg.solve_triangular(factor, identity, lower=True)  34.9 us
  transfers between devices with their start and end apart: 24, of which 10 were waited for; matrix products, arithmetic and copies ran while one was open for 67% of the time, Pallas kernels for 3%

profile of v1, /device:TPU:0, one launch (start us, length us, event | category | flops | bytes accessed | tf_op | source)
XLA Modules:
  0.0 1369.4 jit_solution(220781998046693675)
XLA Ops:
  91.2 111.9 %collective-permute-done = bf16[64,4096]{1,0:T(8,128)(2,1)} collective-permute-done((bf16[64,4096]{1,0:T(8,128)(2,1)}, bf16[64,4096]{1,0:T(8,128)(2,1)}, u32[]{:S(2)}, u32[]{:S(2)}) %collective-permute-start) | collective-permute-done | bytes 524320 | tf_op jit(solution)/shard_map/ppermute | solution.py:36
  209.0 15.8 %collective-permute-done.2 = bf16[1024,512]{0,1:T(8,128)(2,1)} collective-permute-done((bf16[1024,512]{0,1:T(8,128)(2,1)}, bf16[1024,512]{0,1:T(8,128)(2,1)}, u32[]{:S(2)}, u32[]{:S(2)}) %collective-permute-start.2) | collective-permute-done | bytes 1048608 | tf_op jit(solution)/shard_map/ppermute | solution.py:36
  297.0 11.7 cholesky.462
  308.9 9.8 custom-call.35
  321.3 11.7 cholesky.481
  333.0 10.0 custom-call.36
  344.5 11.7 cholesky.502
  356.3 9.8 custom-call.37
  367.5 11.7 cholesky.519
  385.4 11.9 while.8
  397.3 39.3 %custom-call.38 = f32[4,128,128]{1,2,0:T(8,128)S(1)} custom-call(f32[4,128,128]{2,1,0:T(8,128)S(1)} %get-tuple-element.30), custom_call_target="InvertDiagBlocksLowerTriangular" | custom-call | tf_op jit(solution)/shard_map/jit(_solve_triangular)/triangular_solve | solution.py:32
  491.9 11.7 cholesky.606
  503.8 9.8 custom-call.43
  516.1 11.7 cholesky.625
  527.9 10.2 custom-call.44
  539.7 11.7 cholesky.646
  551.4 9.8 custom-call.45
  562.7 11.9 cholesky.663
  580.2 11.1 while.10
  591.2 39.3 %custom-call.46 = f32[4,128,128]{1,2,0:T(8,128)S(1)} custom-call(f32[4,128,128]{2,1,0:T(8,128)S(1)} %get-tuple-element.32), custom_call_target="InvertDiagBlocksLowerTriangular" | custom-call | tf_op jit(solution)/shard_map/jit(_solve_triangular)/triangular_solve | solution.py:32
  649.1 12.1 cholesky.678
  661.9 10.6 custom-call.47
  676.4 12.5 cholesky.697
  689.6 10.6 custom-call.48
  704.0 12.7 cholesky.718
  717.4 10.6 custom-call.49
  730.3 12.3 cholesky.735
  750.7 14.0 %while.11 = (s32[]{:T(128)}, f32[512,512]{1,0:T(8,128)}, s32[4,2]{0,1:T(2,128)S(1)}, f32[4,128,128]{2,1,0:T(8,128)}, s32[]{:T(128)}) while((s32[]{:T(128)}, f32[512,512]{1,0:T(8,128)}, s32[4,2]{0,1:T(2,128)S(1)}, f32[4,128,128]{2,1,0:T(8,128)}, s32[]{:T(128)}) %tuple.251), condition=%wide.while_cond.clone.2, body=%wide.while_body.clone.2.sunk | while | flops 2 | bytes 132205 | solution.py:32
  764.7 40.8 %custom-call.50 = f32[4,128,128]{1,2,0:T(8,128)} custom-call(f32[4,128,128]{2,1,0:T(8,128)} %get-tuple-element.33), custom_call_target="InvertDiagBlocksLowerTriangular" | custom-call | tf_op jit(solution)/shard_map/jit(_solve_triangular)/triangular_solve | solution.py:32
  812.3 11.8 convert_add_fusion.oth
  826.3 19.5 %shard_map.95.own = f32[1024,4096]{1,0:T(8,128)} custom-call(s32[66]{0:T(128)S(1)} %pad_add_fusion.scal, f32[1024,4096]{1,0:T(8,128)} %convert_add_fusion.1.own, f32[1024,4096]{1,0:T(8,128)} %convert_add_fusion.oth, bf16[1024,512]{1,0:T(8,128)(2,1)S(1)} %copy-done.2, bf16[4096,512]{1,0:T(8,128)(2,1)S(1)} %copy-done.3), custom_call_target="tpu_custom_call", output_to_operand_aliasing={{}: (1, {})} | custom-call | flops 4294967296 | bytes 54525952 | tf_op jit(solution)/shard_map/pallas_call | solution.py:122
  871.5 32.8 %collective-permute-done.6 = f32[1024,512]{0,1:T(8,128)S(1)} collective-permute-done((f32[1024,512]{0,1:T(8,128)S(1)}, f32[1024,512]{0,1:T(8,128)S(1)}, u32[]{:S(2)}, u32[]{:S(2)}) %collective-permute-start.6) | collective-permute-done | bytes 2097184 | tf_op jit(solution)/shard_map/ppermute | solution.py:36
  939.8 11.0 collective-permute-done.8
  957.9 12.5 cholesky.534
  972.2 10.6 custom-call.39
  987.3 12.5 cholesky.553
  1000.6 11.0 custom-call.40
  1016.1 12.5 cholesky.574
  1029.3 10.6 custom-call.41
  1043.1 12.5 cholesky.591
  1065.2 13.6 while.9
  1078.8 40.7 %custom-call.42 = f32[4,128,128]{1,2,0:T(8,128)} custom-call(f32[4,128,128]{2,1,0:T(8,128)} %get-tuple-element.31), custom_call_target="InvertDiagBlocksLowerTriangular" | custom-call | tf_op jit(solution)/shard_map/jit(_solve_triangular)/triangular_solve | solution.py:32
  1136.8 29.3 %fusion.7 = f32[4096,512]{1,0:T(8,128)S(1)} fusion(f32[512,4096]{1,0:T(8,128)} %fusion.139, bf16[4096,512]{0,1:T(8,128)(2,1)} %broadcast_select_fusion, bf16[4096,512]{0,1:T(8,128)(2,1)} %collective-permute-done.21, pred[]{:T(512)S(6)} %eq.199, f32[128,512]{1,0:T(8,128)S(1)} %copy-done.30, f32[128,512]{1,0:T(8,128)S(1)} %copy-done.18, ...), kind=kOutput, calls=%fused_computation.19 | convolution fusion | flops 12891979776 | bytes 26214400 | tf_op jit(solution)/shard_map/dot_general | solution.py:26
  1173.8 33.5 %fusion.5 = f32[4096,512]{1,0:T(8,128)} fusion(f32[4096,512]{0,1:T(8,128)} %fusion.225, f32[512,4096]{1,0:T(8,128)} %fusion.134, bf16[4096,512]{0,1:T(8,128)(2,1)} %collective-permute-done.21, bf16[4096,512]{0,1:T(8,128)(2,1)} %broadcast_select_fusion, pred[]{:T(512)S(6)} %eq.199, f32[128,512]{1,0:T(8,128)S(1)} %copy-done.45, ...), kind=kOutput, calls=%fused_computation.17 | convolution fusion | flops 12894076928 | bytes 34603008 | tf_op jit(solution)/shard_map/dot_general | solution.py:26
  1221.8 16.6 %fusion.3 = f32[4096,512]{1,0:T(8,128)} fusion(f32[4096,512]{1,0:T(8,128)} %fusion.10, f32[4096,512]{1,0:T(8,128)} %fusion.224, bf16[4096,512]{1,0:T(8,128)(2,1)} %param.16, f32[4096,512]{1,0:T(8,128)} %fusion.30, f32[4096,512]{1,0:T(8,128)} %copy-done.4, bf16[64,512]{0,1:T(8,128)(2,1)S(1)} %copy-done.24, bf16[64,4096]{1,0:T(8,128)(2,1)S(1)} %copy-done, ...), kind=kOutput, calls=%fused_computation.14 | convolution fusion | flops 285212672 | bytes 46735360 | tf_op jit(solution)/shard_map/dot_general | solution.py:18
  1238.5 9.3 shard_map.96.own
  1265.6 9.3 shard_map.98.own
  1274.9 78.2 %collective-permute-done.11.oth = f32[256,4096]{1,0:T(8,128)} collective-permute-done((f32[256,4096]{1,0:T(8,128)}, f32[256,4096]{1,0:T(8,128)}, u32[]{:S(2)}, u32[]{:S(2)}) %collective-permute-start.11) | collective-permute-done | bytes 4194336 | tf_op jit(solution)/shard_map/ppermute | solution.py:36
  (497 shorter events, 449.6 us)
Async XLA Ops:
  7.2 12.3 copy-start
  7.2 816.9 %all-gather.3.cloned.1.call-start = ((), (), s32[]{:S(2)}) async-start(), calls=%async_computation | async-start | bytes 5242880 | tf_op jit(solution)/shard_map/all_gather | solution.py:228
  7.2 805.0 %collective-permute-start.1 = (bf16[1024,4096]{1,0:T(8,128)(2,1)}, bf16[1024,4096]{1,0:T(8,128)(2,1)}, u32[]{:S(2)}, u32[]{:S(2)}) collective-permute-start(bf16[1024,4096]{1,0:T(8,128)(2,1)} %bitcast.380), channel_id=1, source_target_pairs={{0,4},{4,0},{8,12},{12,8},{16,20},{20,16},{24,28},{28,24},{1,5},{5... | collective-permute-start | bytes 25165832 | tf_op jit(solution)/shard_map/ppermute | solution.py:36
  10.3 192.8 %collective-permute-start = (bf16[64,4096]{1,0:T(8,128)(2,1)}, bf16[64,4096]{1,0:T(8,128)(2,1)}, u32[]{:S(2)}, u32[]{:S(2)}) collective-permute-start(bf16[64,4096]{1,0:T(8,128)(2,1)} %bitcast.391), channel_id=1, source_target_pairs={{0,4},{4,0},{8,12},{12,8},{16,20},{20,16},{24,28},{28,24},{1,5},{5... | collective-permute-start | bytes 1572872 | tf_op jit(solution)/shard_map/ppermute | solution.py:36
  16.4 14.7 %copy-start.49 = (bf16[1,1024,128]{1,2,0:T(8,128)(2,1)}, bf16[1,1024,128]{1,2,0:T(8,128)(2,1)S(1)}, u32[]{:S(2)}) copy-start(bf16[1,1024,128]{1,2,0:T(8,128)(2,1)S(1)} %copy.60) | copy-start | bytes 786436
  17.5 207.2 %collective-permute-start.2 = (bf16[1024,512]{0,1:T(8,128)(2,1)}, bf16[1024,512]{0,1:T(8,128)(2,1)}, u32[]{:S(2)}, u32[]{:S(2)}) collective-permute-start(bf16[1024,512]{0,1:T(8,128)(2,1)} %pad_maximum_fusion.2), channel_id=1, source_target_pairs={{0,4},{4,0},{8,12},{12,8},{16,20},{20,16},{24,28},{28,24},{1,5},{5... | collective-permute-start | bytes 3145736 | tf_op jit(solution)/shard_map/ppermute | solution.py:36
  19.6 250.9 %collective-permute-start.15 = (bf16[64,512]{0,1:T(8,128)(2,1)S(1)}, bf16[64,512]{0,1:T(8,128)(2,1)}, u32[]{:S(2)}, u32[]{:S(2)}) collective-permute-start(bf16[64,512]{0,1:T(8,128)(2,1)S(1)} %copy.129), channel_id=1, source_target_pairs={{0,16},{1,17},{2,18},{3,19}} | collective-permute-start | bytes 196616 | tf_op jit(solution)/shard_map/ppermute | solution.py:59
  31.1 443.8 %collective-permute-start.20 = (bf16[4096,512]{0,1:T(8,128)(2,1)}, bf16[4096,512]{0,1:T(8,128)(2,1)}, u32[]{:S(2)}, u32[]{:S(2)}) collective-permute-start(bf16[4096,512]{0,1:T(8,128)(2,1)} %copy.78), channel_id=1, source_target_pairs={{0,2},{1,3},{4,6},{5,7},{8,10},{9,11},{12,14},{13,15},{16,18},{17,... | collective-permute-start | bytes 12582920 | tf_op jit(solution)/shard_map/ppermute | solution.py:70
  38.3 13.7 %copy-start.57 = (s32[32]{0:T(128)}, s32[32]{0:T(128)S(1)}, u32[]{:S(2)}) copy-start(s32[32]{0:T(128)S(1)} %get-tuple-element.35) | copy-start | bytes 388
  38.3 13.7 %copy-start.60 = (s32[32]{0:T(128)}, s32[32]{0:T(128)S(1)}, u32[]{:S(2)}) copy-start(s32[32]{0:T(128)S(1)} %get-tuple-element.37) | copy-start | bytes 388
  53.6 30.0 %copy-start.25 = (f32[1024,512]{0,1:T(8,128)}, f32[1024,512]{0,1:T(8,128)S(1)}, u32[]{:S(2)}) copy-start(f32[1024,512]{0,1:T(8,128)S(1)} %convert_add_fusion.3) | copy-start | bytes 6291460
  83.5 119.5 %copy-start.47 = (bf16[1024,512]{0,1:T(8,128)(2,1)S(1)}, bf16[1024,512]{0,1:T(8,128)(2,1)}, u32[]{:S(2)}) copy-start(bf16[1024,512]{0,1:T(8,128)(2,1)} %slice.577) | copy-start | bytes 3145732
  85.1 149.9 %slice-start.4 = ((s8[8388608]{0:T(1024)(128)(4,1)}), s8[4194304]{0:T(1024)(128)(4,1)S(1)}, s32[]{:S(2)}) async-start(s8[8388608]{0:T(1024)(128)(4,1)} %bitcast.381), calls=%async_computation.6 | async-start | bytes 8388608
  203.1 41.6 %collective-permute-start.12 = (bf16[1024,512]{0,1:T(8,128)(2,1)S(1)}, bf16[1024,512]{0,1:T(8,128)(2,1)S(1)}, u32[]{:S(2)}, u32[]{:S(2)}) collective-permute-start(bf16[1024,512]{0,1:T(8,128)(2,1)S(1)} %copy-done.47), channel_id=1, source_target_pairs={{0,16},{1,17},{2,18},{3,19}} | collective-permute-start | bytes 3145736 | tf_op jit(solution)/shard_map/ppermute | solution.py:59
  234.8 32.8 %collective-permute-start.3 = (f32[512,512]{0,1:T(8,128)S(1)}, f32[512,512]{0,1:T(8,128)}, u32[]{:S(2)}, u32[]{:S(2)}) collective-permute-start(f32[512,512]{0,1:T(8,128)S(1)} %maximum_add_fusion), channel_id=1, source_target_pairs={{0,1},{1,0},{2,3},{3,2},{4,5},{5,4},{6,7},{7,6},{8,9},{9,8},{10,11... | collective-permute-start | bytes 3145736 | tf_op jit(solution)/shard_map/ppermute | solution.py:36
  244.7 22.9 %copy-start.59 = (s32[32]{0:T(128)S(1)}, s32[32]{0:T(128)}, u32[]{:S(2)}) copy-start(s32[32]{0:T(128)} %copy-done.57) | copy-start | bytes 388
  244.7 22.9 %copy-start.62 = (s32[32]{0:T(128)S(1)}, s32[32]{0:T(128)}, u32[]{:S(2)}) copy-start(s32[32]{0:T(128)} %copy-done.60) | copy-start | bytes 388
  247.1 32.5 %collective-permute-start.13 = (bf16[1024,512]{0,1:T(8,128)(2,1)}, bf16[1024,512]{0,1:T(8,128)(2,1)}, u32[]{:S(2)}, u32[]{:S(2)}) collective-permute-start(bf16[1024,512]{0,1:T(8,128)(2,1)} %broadcast_select_fusion.4), channel_id=1, source_target_pairs={{0,8},{16,24},{1,9},{17,25},{2,10},{18,26},{3,11},{19,27}} | collective-permute-start | bytes 3145736 | tf_op jit(solution)/shard_map/ppermute | solution.py:59
  259.9 17.2 %copy-start.64 = (s32[32]{0:T(128)S(1)}, s32[32]{0:T(128)}, u32[]{:S(2)}) copy-start(s32[32]{0:T(128)} %copy-done.63) | copy-start | bytes 388
  259.9 17.2 %copy-start.66 = (s32[32]{0:T(128)S(1)}, s32[32]{0:T(128)}, u32[]{:S(2)}) copy-start(s32[32]{0:T(128)} %copy-done.65) | copy-start | bytes 388
  269.0 24.1 %collective-permute-start.4 = (f32[512,512]{0,1:T(8,128)S(1)}, f32[512,512]{0,1:T(8,128)S(1)}, u32[]{:S(2)}, u32[]{:S(2)}) collective-permute-start(f32[512,512]{0,1:T(8,128)S(1)} %add.458), channel_id=1, source_target_pairs={{0,2},{1,3},{2,0},{3,1},{4,6},{5,7},{6,4},{7,5},{8,10},{9,11},{10,... | collective-permute-start | bytes 3145736 | tf_op jit(solution)/shard_map/ppermute | solution.py:36
  270.6 5.1 collective-permute-start.16
  275.7 3.8 collective-permute-start.17
  279.5 191.6 %copy-start.22 = (bf16[64,512]{0,1:T(8,128)(2,1)}, bf16[64,512]{0,1:T(8,128)(2,1)S(1)}, u32[]{:S(2)}) copy-start(bf16[64,512]{0,1:T(8,128)(2,1)S(1)} %broadcast_select_fusion.9) | copy-start | bytes 196612
  281.9 154.8 %collective-permute-start.14 = (bf16[1024,512]{0,1:T(8,128)(2,1)}, bf16[1024,512]{0,1:T(8,128)(2,1)}, u32[]{:S(2)}, u32[]{:S(2)}) collective-permute-start(bf16[1024,512]{0,1:T(8,128)(2,1)} %broadcast_select_fusion.5), channel_id=1, source_target_pairs={{0,4},{8,12},{16,20},{24,28},{1,5},{9,13},{17,21},{25,29},{2,6},{1... | collective-permute-start | bytes 3145736 | tf_op jit(solution)/shard_map/ppermute | solution.py:59
  442.9 25.8 %collective-permute-start.18 = (bf16[1088,512]{1,0:T(8,128)(2,1)}, bf16[1088,512]{1,0:T(8,128)(2,1)}, u32[]{:S(2)}, u32[]{:S(2)}) collective-permute-start(bf16[1088,512]{1,0:T(8,128)(2,1)} %copy.80), channel_id=1, source_target_pairs={{0,2},{1,3},{4,6},{5,7},{8,10},{9,11},{12,14},{13,15},{16,18},{17,... | collective-permute-start | bytes 3342344 | tf_op jit(solution)/shard_map/ppermute | solution.py:70
  463.2 775.3 %all-gather.5.cloned.1.call-start = ((), (), s32[]{:S(2)}) async-start(), calls=%async_computation.1 | async-start | bytes 5242880 | tf_op jit(solution)/shard_map/all_gather | solution.py:228
  474.9 5.2 collective-permute-start.19
  479.6 657.1 %collective-permute-start.21 = (bf16[4096,512]{0,1:T(8,128)(2,1)}, bf16[4096,512]{0,1:T(8,128)(2,1)}, u32[]{:S(2)}, u32[]{:S(2)}) collective-permute-start(bf16[4096,512]{0,1:T(8,128)(2,1)} %broadcast_select_fusion), channel_id=1, source_target_pairs={{0,1},{1,0},{2,3},{3,2},{4,5},{5,4},{6,7},{7,6},{8,9},{9,8},{10,11... | collective-permute-start | bytes 12582920 | tf_op jit(solution)/shard_map/ppermute | solution.py:36
  574.6 57.9 %copy-start.8 = (f32[512,512]{1,0:T(8,128)}, f32[512,512]{1,0:T(8,128)S(1)}, u32[]{:S(2)}) copy-start(f32[512,512]{1,0:T(8,128)S(1)} %get-tuple-element.131) | copy-start | bytes 3145732
  747.4 60.8 %copy-start.6 = (f32[512,512]{1,0:T(8,128)}, f32[512,512]{1,0:T(8,128)S(1)}, u32[]{:S(2)}) copy-start(f32[512,512]{1,0:T(8,128)S(1)} %get-tuple-element.121) | copy-start | bytes 3145732
  856.6 47.6 %collective-permute-start.6 = (f32[1024,512]{0,1:T(8,128)S(1)}, f32[1024,512]{0,1:T(8,128)S(1)}, u32[]{:S(2)}, u32[]{:S(2)}) collective-permute-start(f32[1024,512]{0,1:T(8,128)S(1)} %pad_maximum_fusion), channel_id=1, source_target_pairs={{0,8},{4,12},{8,0},{12,4},{16,24},{20,28},{24,16},{28,20},{1,9},{5... | collective-permute-start | bytes 6291464 | tf_op jit(solution)/shard_map/ppermute | solution.py:36
  857.2 58.6 %copy-start.31 = (f32[128,512]{1,0:T(8,128)}, f32[128,512]{1,0:T(8,128)S(1)}, u32[]{:S(2)}) copy-start(f32[128,512]{1,0:T(8,128)S(1)} %fusion.142) | copy-start | bytes 786436
  871.5 41.0 %copy-start.40 = (f32[1024,512]{0,1:T(8,128)}, f32[1024,512]{0,1:T(8,128)S(1)}, u32[]{:S(2)}) copy-start(f32[1024,512]{0,1:T(8,128)S(1)} %get-tuple-element.101) | copy-start | bytes 6291460
  912.5 21.3 %slice-start = ((s8[16777216]{0:T(1024)(128)(4,1)}), s8[4194304]{0:T(1024)(128)(4,1)S(1)}, s32[]{:S(2)}) async-start(s8[16777216]{0:T(1024)(128)(4,1)} %bitcast.377), calls=%async_computation.2 | async-start | bytes 8388608
  912.6 11.6 collective-permute-start.7
  915.8 17.9 %slice-start.1 = ((s8[16777216]{0:T(1024)(128)(4,1)}), s8[4194304]{0:T(1024)(128)(4,1)S(1)}, s32[]{:S(2)}) async-start(s8[16777216]{0:T(1024)(128)(4,1)} %bitcast.377), calls=%async_computation.3 | async-start | bytes 8388608
  918.5 15.2 %slice-start.2 = ((s8[16777216]{0:T(1024)(128)(4,1)}), s8[4194304]{0:T(1024)(128)(4,1)S(1)}, s32[]{:S(2)}) async-start(s8[16777216]{0:T(1024)(128)(4,1)} %bitcast.377), calls=%async_computation.4 | async-start | bytes 8388608
  924.4 26.4 %collective-permute-start.8 = (f32[512,512]{0,1:T(8,128)S(1)}, f32[512,512]{0,1:T(8,128)S(1)}, u32[]{:S(2)}, u32[]{:S(2)}) collective-permute-start(f32[512,512]{0,1:T(8,128)S(1)} %add.493), channel_id=1, source_target_pairs={{0,2},{1,3},{2,0},{3,1},{4,6},{5,7},{6,4},{7,5},{8,10},{9,11},{10,... | collective-permute-start | bytes 3145736 | tf_op jit(solution)/shard_map/ppermute | solution.py:36
  933.7 17.0 %copy-start.67 = (f32[1,512]{1,0:T(1,128)S(1)}, f32[1,512]{1,0:T(1,128)}, u32[]{:S(2)}) copy-start(f32[1,512]{1,0:T(1,128)} %get-tuple-element.160) | copy-start | bytes 6148
  937.8 234.0 %collective-permute-start.5 = (f32[256,4096]{1,0:T(8,128)}, f32[256,4096]{1,0:T(8,128)}, u32[]{:S(2)}, u32[]{:S(2)}) collective-permute-start(f32[256,4096]{1,0:T(8,128)} %get-tuple-element.81), channel_id=1, source_target_pairs={{0,8},{4,12},{8,0},{12,4},{16,24},{20,28},{24,16},{28,20},{1,9},{5... | collective-permute-start | bytes 12582920 | tf_op jit(solution)/shard_map/ppermute | solution.py:36
  938.1 233.7 %collective-permute-start.9 = (f32[256,4096]{1,0:T(8,128)}, f32[256,4096]{1,0:T(8,128)}, u32[]{:S(2)}, u32[]{:S(2)}) collective-permute-start(f32[256,4096]{1,0:T(8,128)} %get-tuple-element.80), channel_id=1, source_target_pairs={{0,8},{4,12},{8,0},{12,4},{16,24},{20,28},{24,16},{28,20},{1,9},{5... | collective-permute-start | bytes 12582920 | tf_op jit(solution)/shard_map/ppermute | solution.py:36
  1136.7 29.3 %copy-start.9 = (f32[512,512]{1,0:T(8,128)S(1)}, f32[512,512]{1,0:T(8,128)}, u32[]{:S(2)}) copy-start(f32[512,512]{1,0:T(8,128)} %copy-done.8) | copy-start | bytes 3145732
  1166.3 43.4 %copy-start.4 = (f32[4096,512]{1,0:T(8,128)}, f32[4096,512]{1,0:T(8,128)S(1)}, u32[]{:S(2)}) copy-start(f32[4096,512]{1,0:T(8,128)S(1)} %fusion.31) | copy-start | bytes 25165828
  1171.8 35.5 %copy-start.7 = (f32[512,512]{1,0:T(8,128)S(1)}, f32[512,512]{1,0:T(8,128)}, u32[]{:S(2)}) copy-start(f32[512,512]{1,0:T(8,128)} %copy-done.6) | copy-start | bytes 3145732
  1171.8 93.8 %collective-permute-start.10 = (f32[256,4096]{1,0:T(8,128)}, f32[256,4096]{1,0:T(8,128)}, u32[]{:S(2)}, u32[]{:S(2)}) collective-permute-start(f32[256,4096]{1,0:T(8,128)} %collective-permute-done.5.oth), channel_id=1, source_target_pairs={{0,4},{4,0},{8,12},{12,8},{16,20},{20,16},{24,28},{28,24},{1,5},{5... | collective-permute-start | bytes 12582920 | tf_op jit(solution)/shard_map/ppermute | solution.py:36
  1171.8 181.3 %collective-permute-start.11 = (f32[256,4096]{1,0:T(8,128)}, f32[256,4096]{1,0:T(8,128)}, u32[]{:S(2)}, u32[]{:S(2)}) collective-permute-start(f32[256,4096]{1,0:T(8,128)} %collective-permute-done.9.oth), channel_id=1, source_target_pairs={{0,4},{4,0},{8,12},{12,8},{16,20},{20,16},{24,28},{28,24},{1,5},{5... | collective-permute-start | bytes 12582920 | tf_op jit(solution)/shard_map/ppermute | solution.py:36
  1221.8 16.6 %copy-start.1 = (bf16[1024,512]{1,0:T(8,128)(2,1)S(1)}, bf16[1024,512]{1,0:T(8,128)(2,1)}, u32[]{:S(2)}) copy-start(bf16[1024,512]{1,0:T(8,128)(2,1)} %fusion.24.lrow) | copy-start | bytes 3145732
  (50 other events, 209.4 us)
Sparse Core Ops, SparseCore 0:
  463.3 32.7 all-gather.2
  1136.9 34.2 all-gather.4

commit v2 on v1

--- a/solution.py
+++ b/solution.py
@@ -23,13 +23,29 @@
 
 
 def solved(rows, inverse):
-    return lax.dot_general(rows, inverse, LAST, precision=HIGH, preferred_element_type=jnp.float32)
-
-
-def factor_inverse(block):
-    factor = jnp.linalg.cholesky(block)
-    identity = jnp.eye(block.shape[0], dtype=jnp.float32)
-    return factor, jax.scipy.linalg.solve_triangular(factor, identity, lower=True)
+    return jnp.dot(rows, inverse, precision=HIGH, preferred_element_type=jnp.float32)
+
+
+def inverse_factor(block):
+    order = block.shape[0]
+    small = jnp.eye(BS, dtype=jnp.float32)
+    rest = jnp.concatenate([block, jnp.eye(order, dtype=jnp.float32)], axis=0)
+    columns = []
+    for at in range(0, order, BS):
+        factor = jnp.linalg.cholesky(rest[at : at + BS, :BS])
+        inverse = jax.scipy.linalg.solve_triangular(factor, small, lower=True)
+        column = solved(rest[:, :BS], inverse.T)
+        columns.append(column[order:])
+        if at + BS < order:
+            rest = rest[:, BS:] - solved(column, column[at + BS : order].T)
+    return jnp.concatenate(columns, axis=1)
+
+
+def inverse_pair(tree_block, top_block):
+    low = (lax.axis_index("blk") // 2) % 2 == 0
+    mine = inverse_factor(jnp.where(low, tree_block, top_block))
+    mate = swapped(mine, "blk", 2)
+    return jnp.where(low, mine, mate), jnp.where(low, mate, mine)
 
 
 def swapped(value, axis, mask):
@@ -162,44 +178,6 @@
     return below, pivot
 
 
-def top_part(top_net, top_coupling):
-    leaf_pos, blk_pos = lax.axis_index("leaf"), lax.axis_index("blk")
-    rows_top = top_net.shape[1]
-    lead = 2 * PW
-    coup0, coup1 = first_two(top_coupling)
-    piece = lax.dynamic_slice_in_dim(top_net, (blk_pos * PW) % rows_top, PW, 1)
-    net_mine = leaf_spread(piece, lambda b: (b * PW) // rows_top)
-    lead_mine = leaf_spread(top_coupling[:lead], lambda b: 0)
-    both0, both1 = first_two(jnp.concatenate([lead_mine, net_mine], axis=0))
-    lead0, net0 = both0[:lead].astype(jnp.float32), both0[lead:]
-    lead1, net1 = both1[:lead].astype(jnp.float32), both1[lead:]
-    mine = lead_mine.astype(jnp.float32)
-    factor0, inv0 = factor_inverse(gram(net0, net0) + lead0[:PW])
-    cross = solved(gram(net1, net0) + lead0[PW:], inv0).astype(jnp.bfloat16)
-    factor1, inv1 = factor_inverse(gram(net1, net1) + lead1[PW:] - outer(cross, cross))
-    q0 = solved((gram(net0, net_mine) + mine[:PW]).T, inv0).astype(jnp.bfloat16)
-    q1 = solved((gram(net1, net_mine) + mine[PW:]).T - outer(q0, cross), inv1)
-    q1 = q1.astype(jnp.bfloat16)
-    holds = leaf_pos == 0
-    row = (leaf_pos * rows_top + jnp.arange(rows_top, dtype=jnp.int32))[:, None]
-
-    def panel(current, inverse, factor, first):
-        full = solved(current, inverse)
-        placed = lax.dynamic_update_slice(full, factor, (first, 0))
-        full = jnp.where(holds, placed, full)
-        return jnp.where(row >= first, full, 0.0)
-
-    p0 = panel(gram(top_net, net0) + coup0.astype(jnp.float32), inv0, factor0, 0)
-    b0 = p0.astype(jnp.bfloat16)
-    p1 = panel(
-        gram(top_net, net1) + coup1.astype(jnp.float32) - outer(b0, cross), inv1, factor1, PW
-    )
-    b1 = p1.astype(jnp.bfloat16)
-    rest = gram(top_net, net_mine) + top_coupling.astype(jnp.float32)
-    rest = rest - outer(b0, q0) - outer(b1, q1)
-    return jnp.where(blk_pos == 0, p0, jnp.where(blk_pos == 1, p1, rest))
-
-
 def per_device(leaf_net, leaf_coupling, index_maps, sep_anchor, top_net, top_coupling):
     leaf_count = lax.axis_size("leaf")
     leaf_pos, blk_pos = lax.axis_index("leaf"), lax.axis_index("blk")
@@ -219,24 +197,47 @@
         row = lax.dynamic_index_in_dim(index_maps, base + node, 0, keepdims=False)
         return sources(row, 0, sep_blocks), sources(row, sep_blocks, upd_blocks)
 
-    def factor_columns(cols_own, cols_oth, own, oth, anchor):
+    def columns_and_pivot(cols_own, cols_oth, own, oth, anchor):
         below_a, pivot_a = front_columns(cols_own, own[1], own[0], block_first, block_rows)
         below_b, pivot_b = front_columns(cols_oth, oth[1], oth[0], block_first, block_rows)
-        pivot = total(pivot_a + pivot_b, "blk") + jnp.diag(anchor)
-        inverse = factor_inverse(pivot)[1]
-        lrow = solved(below_a + below_b, inverse).astype(jnp.bfloat16)
+        return below_a + below_b, total(pivot_a + pivot_b, "blk") + jnp.diag(anchor)
+
+    def eliminated(below, inverse):
+        lrow = solved(below, inverse).astype(jnp.bfloat16)
         return lrow, lax.all_gather(lrow, "blk", axis=0, tiled=True)
+
+    rows_top = top_net.shape[1]
+    lead = 2 * PW
+    row = (leaf_pos * rows_top + jnp.arange(rows_top, dtype=jnp.int32))[:, None]
+    col = jnp.arange(PW, dtype=jnp.int32)[None, :]
+
+    def panel(current, inverse, first):
+        return jnp.where(row - first >= col, solved(current, inverse), 0.0)
 
     own, oth = maps(0, leaf_pos), maps(0, leaf_pos ^ 1)
     net_oth = swapped(net_own, "leaf", 1)
     coup_cols = take_columns(coup_own, own[0])
     coup_cols_oth = swapped(coup_cols, "leaf", 1)
+    piece = lax.dynamic_slice_in_dim(top_net, (blk_pos * PW) % rows_top, PW, 1)
+    net_mine = leaf_spread(piece, lambda b: (b * PW) // rows_top)
+    lead_mine = leaf_spread(top_coupling[:lead], lambda b: 0)
+    net_oth, coup_cols_oth, lead_mine, net_mine, coup_own = lax.optimization_barrier(
+        (net_oth, coup_cols_oth, lead_mine, net_mine, coup_own)
+    )
     coup_oth = swapped(coup_own, "leaf", 1)
+    both0, both1 = first_two(jnp.concatenate([lead_mine, net_mine], axis=0))
+    both0, both1, top_late = lax.optimization_barrier((both0, both1, top_coupling))
+    coup0, coup1 = first_two(top_late)
+    lead0, net0 = both0[:lead].astype(jnp.float32), both0[lead:]
+    lead1, net1 = both1[:lead].astype(jnp.float32), both1[lead:]
+    mine = lead_mine.astype(jnp.float32)
     cols_own = gram(my_part(net_own), take_columns(net_own, own[0])) + coup_cols.astype(jnp.float32)
     cols_oth = gram(my_part(net_oth), take_columns(net_oth, oth[0])) + coup_cols_oth.astype(
         jnp.float32
     )
-    lrow, lall = factor_columns(cols_own, cols_oth, own, oth, sep_anchor[leaf_pos >> 1])
+    below, pivot = columns_and_pivot(cols_own, cols_oth, own, oth, sep_anchor[leaf_pos >> 1])
+    inverse, inv0 = inverse_pair(pivot, gram(net0, net0) + lead0[:PW])
+    lrow, lall = eliminated(below, inverse)
     u_own = gram(my_part(net_own), net_own) + coup_own.astype(jnp.float32)
     u_oth = gram(my_part(net_oth), net_oth) + coup_oth.astype(jnp.float32)
     update = merge(0, block_first, own[1], oth[1], u_own, u_oth, lrow, lall)
@@ -261,8 +262,22 @@
     else:
         pieces = [(0, swapped(update, "leaf", 2))]
     anchor = sep_anchor[leaf_count // 2 + (node >> 1)]
-    lrow, lall = factor_columns(cols_own, cols_oth, own, oth, anchor)
-    window = top_part(top_net, top_coupling)
+    below, pivot = columns_and_pivot(cols_own, cols_oth, own, oth, anchor)
+    cross = solved(gram(net1, net0) + lead0[PW:], inv0).astype(jnp.bfloat16)
+    inverse, inv1 = inverse_pair(
+        pivot, gram(net1, net1) + lead1[PW:] - outer(cross, cross)
+    )
+    lrow, lall = eliminated(below, inverse)
+    q0 = solved((gram(net0, net_mine) + mine[:PW]).T, inv0).astype(jnp.bfloat16)
+    q1 = solved((gram(net1, net_mine) + mine[PW:]).T - outer(q0, cross), inv1)
+    q1 = q1.astype(jnp.bfloat16)
+    p0 = panel(gram(top_net, net0) + coup0.astype(jnp.float32), inv0, 0)
+    b0 = p0.astype(jnp.bfloat16)
+    x1 = gram(top_net, net1) + coup1.astype(jnp.float32) - outer(b0, cross)
+    p1 = panel(x1, inv1, PW)
+    rest = gram(top_net, net_mine) + top_coupling.astype(jnp.float32) - outer(b0, q0)
+    rest = rest - outer(p1.astype(jnp.bfloat16), q1)
+    window = jnp.where(blk_pos == 0, p0, jnp.where(blk_pos == 1, p1, rest))
     for at, piece in pieces:
         update = merge(at, block_first, own[1], oth[1], update, piece, lrow, lall)
     return (update[None], window)

time: 1380 us -> 907 us (0.66)
  other arithmetic: 574 us -> 266 us
  local copies, waits for them, and re-layouts: 127 us -> 69.9 us
  waiting for transfers between devices: 275 us -> 220 us
  matrix products: 224 us -> 185 us
    another operation x68 -> x40, other arithmetic: 500 us -> 184 us  [the longest x24 99.8 us: inverse_factor(): factor = jnp.linalg.cholesky(rest[at:at + BS, :BS])]
    ppermute x14 -> x16, waiting for transfers between devices: 264 us -> 159 us  [swapped(): lax.ppermute(value, axis, [(s, s ^ mask) for s in range(lax.axis_size(axi...]
    another operation x52 -> x8, matrix products: 62.6 us -> 2.28 us  [inverse_factor(): inverse = jax.scipy.linalg.solve_triangular(factor, small, lower=True)]
    another operation x69 -> x0, local copies, waits for them, and re-layouts: 56.6 us -> none  [the longest x53 51.9 us: factor_inverse(): jax.scipy.linalg.solve_triangular(factor, identity, lower=True)]
    ppermute x2, waiting for transfers between devices: 5.42 us -> 40.1 us  [first_two(): got = lax.ppermute(value, 'blk', [(s, s + step) for s in range(step)])]
    dot_general x7 -> x21, matrix products: 86.3 us -> 102 us  [solved(): jnp.dot(rows, inverse, precision=HIGH, preferred_element_type=jnp.float32)]
    ppermute x6, waiting for transfers between devices: 6.19 us -> 20.7 us  [leaf_spread(): got = lax.ppermute(value, ('leaf', 'blk'), pairs)]
    unnamed x30 -> x29, other arithmetic: 24.2 us -> 31.6 us
  transfers between devices with their start and end apart: 24 -> 26, of which waited for: 10 -> 13; matrix products, arithmetic and copies ran while one was open for 67% -> 54% of each run, Pallas kernels for 3% -> 3%
where the time goes in v2:
time: 907 us; the launch traced here: 898 us
  other arithmetic  266 us (29%)
  waiting for transfers between devices  220 us (24%)
  matrix products  185 us (20%)
  local copies, waits for them, and re-layouts  69.9 us (8%)
  Pallas kernels  56.2 us (6%)
  between operations  54 us (6%)
  starting transfers between devices  45.7 us (5%)
    ppermute x16, waiting for transfers between devices, swapped(): lax.ppermute(value, axis, [(s, s ^ mask) for s in range(lax.axis_size(axi...  159 us
    dot_general x21, matrix products, solved(): jnp.dot(rows, inverse, precision=HIGH, preferred_element_type=jnp.float32)  102 us
    another operation x24, other arithmetic, inverse_factor(): factor = jnp.linalg.cholesky(rest[at:at + BS, :BS])  99.8 us
    another operation x16, other arithmetic, inverse_factor(): inverse = jax.scipy.linalg.solve_triangular(factor, small, lower=True)  83.9 us
    dot_general x12, matrix products, gram(): lax.dot_general(left, right, FIRST, preferred_element_type=jnp.float32)  61.9 us
    pallas_call x5, Pallas kernels, merge(): pl.pallas_call(merge_kernel, out_shape=jax.ShapeDtypeStruct(own.shape, jn...  56.2 us
    ppermute x2, waiting for transfers between devices, first_two(): got = lax.ppermute(value, 'blk', [(s, s + step) for s in range(step)])  40.1 us
    unnamed x29, other arithmetic  31.6 us
  transfers between devices with their start and end apart: 26, of which 13 were waited for; matrix products, arithmetic and copies ran while one was open for 54% of the time, Pallas kernels for 3%

profile of v2, /device:TPU:0, one launch (start us, length us, event | category | flops | bytes accessed | tf_op | source)
XLA Modules:
  0.0 897.7 jit_solution(15450475580754016216)
XLA Ops:
  19.5 4.6 collective-permute-start.2
  59.9 11.5 %collective-permute-done.3 = bf16[1024,512]{0,1:T(8,128)(2,1)S(1)} collective-permute-done((bf16[1024,512]{0,1:T(8,128)(2,1)S(1)}, bf16[1024,512]{0,1:T(8,128)(2,1)S(1)}, u32[]{:S(2)}, u32[]{:S(2)}) %collective-permute-start.3) | collective-permute-done | bytes 1048608 | tf_op jit(solution)/shard_map/ppermute | solution.py:75
  116.6 9.5 %collective-permute-done.11 = bf16[1088,512]{1,0:T(8,128)(2,1)S(1)} collective-permute-done((bf16[1088,512]{1,0:T(8,128)(2,1)}, bf16[1088,512]{1,0:T(8,128)(2,1)S(1)}, u32[]{:S(2)}, u32[]{:S(2)}) %collective-permute-start.11) | collective-permute-done | bytes 1114144 | tf_op jit(solution)/shard_map/ppermute | solution.py:86
  147.7 17.1 %collective-permute-done.10 = f32[512,512]{0,1:T(8,128)} collective-permute-done((f32[512,512]{0,1:T(8,128)S(1)}, f32[512,512]{0,1:T(8,128)}, u32[]{:S(2)}, u32[]{:S(2)}) %collective-permute-start.10) | collective-permute-done | bytes 1048608 | tf_op jit(solution)/shard_map/ppermute | solution.py:52
  166.5 11.7 %cholesky.134 = f32[128,128]{1,0:T(8,128)S(1)} custom-call(f32[128,128]{1,0:T(8,128)S(1)} %fusion.148), custom_call_target="Cholesky" | custom-call | tf_op jit(solution)/shard_map/jit(cholesky)/cholesky | solution.py:35
  179.6 9.8 %custom-call.12 = f32[1,128,128]{1,2,0:T(8,128)S(1)} custom-call(f32[1,128,128]{2,1,0:T(8,128)S(1)} %fusion.109), custom_call_target="InvertDiagBlocksLowerTriangular" | custom-call | tf_op jit(solution)/shard_map/jit(_solve_triangular)/triangular_solve | solution.py:36
  193.9 12.1 %cholesky.145 = f32[128,128]{1,0:T(8,128)S(1)} custom-call(f32[128,128]{1,0:T(8,128)S(1)} %fusion.146), custom_call_target="Cholesky" | custom-call | tf_op jit(solution)/shard_map/jit(cholesky)/cholesky | solution.py:35
  207.3 9.8 %custom-call.13 = f32[1,128,128]{1,2,0:T(8,128)S(1)} custom-call(f32[1,128,128]{2,1,0:T(8,128)S(1)} %fusion.110), custom_call_target="InvertDiagBlocksLowerTriangular" | custom-call | tf_op jit(solution)/shard_map/jit(_solve_triangular)/triangular_solve | solution.py:36
  222.2 11.7 %cholesky.156 = f32[128,128]{1,0:T(8,128)S(1)} custom-call(f32[128,128]{1,0:T(8,128)S(1)} %fusion.144), custom_call_target="Cholesky" | custom-call | tf_op jit(solution)/shard_map/jit(cholesky)/cholesky | solution.py:35
  235.2 9.8 %custom-call.14 = f32[1,128,128]{1,2,0:T(8,128)S(1)} custom-call(f32[1,128,128]{2,1,0:T(8,128)S(1)} %fusion.111), custom_call_target="InvertDiagBlocksLowerTriangular" | custom-call | tf_op jit(solution)/shard_map/jit(_solve_triangular)/triangular_solve | solution.py:36
  248.6 11.7 %cholesky.167 = f32[128,128]{1,0:T(8,128)S(1)} custom-call(f32[128,128]{1,0:T(8,128)S(1)} %fusion.142), custom_call_target="Cholesky" | custom-call | tf_op jit(solution)/shard_map/jit(cholesky)/cholesky | solution.py:35
  261.6 9.8 %custom-call.15 = f32[1,128,128]{1,2,0:T(8,128)S(1)} custom-call(f32[1,128,128]{2,1,0:T(8,128)S(1)} %fusion.112), custom_call_target="InvertDiagBlocksLowerTriangular" | custom-call | tf_op jit(solution)/shard_map/jit(_solve_triangular)/triangular_solve | solution.py:36
  275.1 23.0 %collective-permute-done.13 = f32[512,512]{0,1:T(8,128)S(1)} collective-permute-done((f32[512,512]{0,1:T(8,128)S(1)}, f32[512,512]{0,1:T(8,128)S(1)}, u32[]{:S(2)}, u32[]{:S(2)}) %collective-permute-start.13) | collective-permute-done | bytes 1048608 | tf_op jit(solution)/shard_map/ppermute | solution.py:52
  299.2 9.6 %fusion.28.lrow = bf16[1024,512]{1,0:T(8,128)(2,1)} fusion(f32[1024,512]{0,1:T(8,128)S(1)} %copy-done.38, f32[1024,512]{0,1:T(8,128)} %copy-done.39, f32[512,512]{0,1:T(8,128)S(1)} %collective-permute-done.13, pred[]{:T(512)S(6)} %eq.212, f32[512,128]{0,1:T(8,128)S(1)} %fusion.56, f32[512,128]{0,1:T(8,128)S(1)} %slice.637, f32[512,128]{0,1:T(8,128)S(1)} %slice.632, ...), kind=kOutput, calls=%fused_computation.42 | convolution fusion | flops 3223322624 | bytes 7340033 | tf_op jit(solution)/shard_map/dot_general | solution.py:26
  334.4 11.9 %convert_add_fusion.1.own = f32[1024,4096]{1,0:T(8,128)} fusion(bf16[1024,4096]{1,0:T(8,128)(2,1)} %bitcast.277, bf16[1,64,4096]{2,1,0:T(8,128)(2,1)S(1)} %copy-done.51, s32[]{:T(128)S(6)} %select_n.749), kind=kOutput, calls=%fused_computation.1 | convolution fusion | flops 545259520 | bytes 25821188 | tf_op jit(solution)/shard_map/dot_general | solution.py:18
  346.3 11.8 %convert_add_fusion.oth = f32[1024,4096]{1,0:T(8,128)} fusion(bf16[1024,4096]{1,0:T(8,128)(2,1)} %collective-permute-done.8, bf16[64,4096]{1,0:T(8,128)(2,1)} %collective-permute-done, s32[]{:T(128)S(6)} %select_n.749), kind=kOutput, calls=%fused_computation | convolution fusion | flops 545259520 | bytes 25821188 | tf_op jit(solution)/shard_map/dot_general | solution.py:18
  360.3 19.1 %shard_map.95.own = f32[1024,4096]{1,0:T(8,128)} custom-call(s32[66]{0:T(128)S(1)} %pad_add_fusion.scal, f32[1024,4096]{1,0:T(8,128)} %convert_add_fusion.1.own, f32[1024,4096]{1,0:T(8,128)} %convert_add_fusion.oth, bf16[1024,512]{1,0:T(8,128)(2,1)S(1)} %copy-done.2, bf16[4096,512]{1,0:T(8,128)(2,1)S(1)} %copy-done.3), custom_call_target="tpu_custom_call", output_to_operand_aliasing={{}: (1, {})} | custom-call | flops 4294967296 | bytes 54525952 | tf_op jit(solution)/shard_map/pallas_call | solution.py:138
  393.1 6.4 copy.115
  399.5 5.8 collective-permute-start.22
  409.2 5.5 fusion.105
  430.4 7.6 collective-permute-done.15
  449.1 5.0 dynamic-slice_select_fusion.3
  463.7 30.6 %collective-permute-done.22 = bf16[4096,512]{0,1:T(8,128)(2,1)} collective-permute-done((bf16[4096,512]{0,1:T(8,128)(2,1)}, bf16[4096,512]{0,1:T(8,128)(2,1)}, u32[]{:S(2)}, u32[]{:S(2)}) %collective-permute-start.22) | collective-permute-done | bytes 4194336 | tf_op jit(solution)/shard_map/ppermute | solution.py:86
  494.3 4.6 broadcast_select_fusion
  504.8 9.1 %collective-permute-done.17 = f32[512,512]{0,1:T(8,128)} collective-permute-done((f32[512,512]{0,1:T(8,128)S(1)}, f32[512,512]{0,1:T(8,128)}, u32[]{:S(2)}, u32[]{:S(2)}) %collective-permute-start.17) | collective-permute-done | bytes 1048608 | tf_op jit(solution)/shard_map/ppermute | solution.py:52
  517.5 11.8 %cholesky.178 = f32[128,128]{1,0:T(8,128)S(1)} custom-call(f32[128,128]{1,0:T(8,128)S(1)} %fusion.140), custom_call_target="Cholesky" | custom-call | tf_op jit(solution)/shard_map/jit(cholesky)/cholesky | solution.py:35
  530.7 9.8 %custom-call.16 = f32[1,128,128]{1,2,0:T(8,128)S(1)} custom-call(f32[1,128,128]{2,1,0:T(8,128)S(1)} %fusion.113), custom_call_target="InvertDiagBlocksLowerTriangular" | custom-call | tf_op jit(solution)/shard_map/jit(_solve_triangular)/triangular_solve | solution.py:36
  546.1 11.7 %cholesky.189 = f32[128,128]{1,0:T(8,128)S(1)} custom-call(f32[128,128]{1,0:T(8,128)S(1)} %fusion.138), custom_call_target="Cholesky" | custom-call | tf_op jit(solution)/shard_map/jit(cholesky)/cholesky | solution.py:35
  559.2 9.8 %custom-call.17 = f32[1,128,128]{1,2,0:T(8,128)S(1)} custom-call(f32[1,128,128]{2,1,0:T(8,128)S(1)} %fusion.114), custom_call_target="InvertDiagBlocksLowerTriangular" | custom-call | tf_op jit(solution)/shard_map/jit(_solve_triangular)/triangular_solve | solution.py:36
  574.3 11.7 %cholesky.200 = f32[128,128]{1,0:T(8,128)S(1)} custom-call(f32[128,128]{1,0:T(8,128)S(1)} %fusion.136), custom_call_target="Cholesky" | custom-call | tf_op jit(solution)/shard_map/jit(cholesky)/cholesky | solution.py:35
  587.3 9.8 %custom-call.18 = f32[1,128,128]{1,2,0:T(8,128)S(1)} custom-call(f32[1,128,128]{2,1,0:T(8,128)S(1)} %fusion.115), custom_call_target="InvertDiagBlocksLowerTriangular" | custom-call | tf_op jit(solution)/shard_map/jit(_solve_triangular)/triangular_solve | solution.py:36
  601.6 11.7 %cholesky.211 = f32[128,128]{1,0:T(8,128)S(1)} custom-call(f32[128,128]{1,0:T(8,128)S(1)} %fusion.134), custom_call_target="Cholesky" | custom-call | tf_op jit(solution)/shard_map/jit(cholesky)/cholesky | solution.py:35
  614.6 10.2 %custom-call.19 = f32[1,128,128]{1,2,0:T(8,128)S(1)} custom-call(f32[1,128,128]{2,1,0:T(8,128)S(1)} %fusion.116), custom_call_target="InvertDiagBlocksLowerTriangular" | custom-call | tf_op jit(solution)/shard_map/jit(_solve_triangular)/triangular_solve | solution.py:36
  632.6 5.6 fusion.100
  641.5 10.6 %collective-permute-done.18 = f32[512,512]{0,1:T(8,128)S(1)} collective-permute-done((f32[512,512]{0,1:T(8,128)S(1)}, f32[512,512]{0,1:T(8,128)S(1)}, u32[]{:S(2)}, u32[]{:S(2)}) %collective-permute-start.18) | collective-permute-done | bytes 1048608 | tf_op jit(solution)/shard_map/ppermute | solution.py:52
  653.1 7.9 fusion.31.lrow
  661.0 28.9 %fusion.7 = f32[4096,512]{1,0:T(8,128)S(1)} fusion(f32[512,512]{0,1:T(8,128)S(1)} %copy-done.7, f32[512,4096]{1,0:T(8,128)} %fusion.105, bf16[4096,512]{0,1:T(8,128)(2,1)} %broadcast_select_fusion, bf16[4096,512]{0,1:T(8,128)(2,1)} %collective-permute-done.23, pred[]{:T(512)S(6)} %eq.214), kind=kOutput, calls=%fused_computation.11 | convolution fusion | flops 12891193344 | bytes 26214400 | tf_op jit(solution)/shard_map/dot_general | solution.py:26
  690.0 6.1 fusion.169
  696.2 5.5 fusion.167
  705.5 30.1 %fusion.5 = f32[4096,512]{1,0:T(8,128)S(1)} fusion(f32[4096,512]{0,1:T(8,128)} %fusion.169, f32[512,4096]{1,0:T(8,128)} %fusion.100, bf16[4096,512]{0,1:T(8,128)(2,1)} %collective-permute-done.23, bf16[4096,512]{0,1:T(8,128)(2,1)} %broadcast_select_fusion, pred[]{:T(512)S(6)} %eq.214, f32[512,512]{0,1:T(8,128)S(1)} %copy-done.12, pred[]{:T(512)S(6)} %eq.212, ...), kind=kOutput, calls=%fused_computation.9 | convolution fusion | flops 12894339072 | bytes 35651584 | tf_op jit(solution)/shard_map/dot_general | solution.py:26
  739.0 5.4 fusion.14
  744.4 17.0 %fusion.3 = f32[4096,512]{1,0:T(8,128)} fusion(f32[4096,512]{1,0:T(8,128)} %fusion.14, f32[4096,512]{1,0:T(8,128)} %fusion.167, bf16[4096,512]{1,0:T(8,128)(2,1)} %param.16, f32[4096,512]{1,0:T(8,128)} %copy-done.5, f32[4096,512]{1,0:T(8,128)} %copy-done.4, bf16[64,512]{0,1:T(8,128)(2,1)S(1)} %broadcast_select_fusion.13, bf16[64,4096]{1,0:T(8,128)(2,1)S(1)} %copy-done, ...), kind=kOutput, calls=%fused_computation.6 | convolution fusion | flops 289406976 | bytes 46759936 | tf_op jit(solution)/shard_map/dot_general | solution.py:18
  761.4 9.3 %shard_map.96.own = f32[1024,4096]{1,0:T(8,128)} custom-call(s32[66]{0:T(128)S(1)} %get-tuple-element.72.scal, f32[1024,4096]{1,0:T(8,128)} %shard_map.95.own, f32[256,4096]{1,0:T(8,128)} %collective-permute-done.14.oth, bf16[1024,512]{1,0:T(8,128)(2,1)S(1)} %copy-done.1, ...), custom_call_target="tpu_custom_call", output_to_operand_aliasing={{}: (1, {})} | custom-call | flops 1073741824 | bytes 16777216 | tf_op jit(solution)/shard_map/pallas_call | solution.py:138
  770.7 9.3 %shard_map.97.own = f32[1024,4096]{1,0:T(8,128)} custom-call(s32[66]{0:T(128)S(1)} %get-tuple-element.74.scal, f32[1024,4096]{1,0:T(8,128)} %shard_map.96.own, f32[256,4096]{1,0:T(8,128)} %collective-permute-done.19.oth, bf16[1024,512]{1,0:T(8,128)(2,1)S(1)} %copy-done.1, ...), custom_call_target="tpu_custom_call", output_to_operand_aliasing={{}: (1, {})} | custom-call | flops 1073741824 | bytes 16777216 | tf_op jit(solution)/shard_map/pallas_call | solution.py:138
  780.0 15.5 %collective-permute-done.20.oth = f32[256,4096]{1,0:T(8,128)} collective-permute-done((f32[256,4096]{1,0:T(8,128)}, f32[256,4096]{1,0:T(8,128)}, u32[]{:S(2)}, u32[]{:S(2)}) %collective-permute-start.20) | collective-permute-done | bytes 4194336 | tf_op jit(solution)/shard_map/ppermute | solution.py:52
  795.4 9.3 %shard_map.98.own = f32[1024,4096]{1,0:T(8,128)} custom-call(s32[66]{0:T(128)S(1)} %get-tuple-element.73.scal, f32[1024,4096]{1,0:T(8,128)} %shard_map.97.own, f32[256,4096]{1,0:T(8,128)} %collective-permute-done.20.oth, bf16[1024,512]{1,0:T(8,128)(2,1)S(1)} %copy-done.1, ...), custom_call_target="tpu_custom_call", output_to_operand_aliasing={{}: (1, {})} | custom-call | flops 1073741824 | bytes 16777216 | tf_op jit(solution)/shard_map/pallas_call | solution.py:138
  804.7 76.4 %collective-permute-done.21.oth = f32[256,4096]{1,0:T(8,128)} collective-permute-done((f32[256,4096]{1,0:T(8,128)}, f32[256,4096]{1,0:T(8,128)}, u32[]{:S(2)}, u32[]{:S(2)}) %collective-permute-start.21) | collective-permute-done | bytes 4194336 | tf_op jit(solution)/shard_map/ppermute | solution.py:52
  881.2 9.3 %shard_map.99 = f32[1024,4096]{1,0:T(8,128)} custom-call(s32[66]{0:T(128)S(1)} %get-tuple-element.75.scal, f32[1024,4096]{1,0:T(8,128)} %shard_map.98.own, f32[256,4096]{1,0:T(8,128)} %collective-permute-done.21.oth, bf16[1024,512]{1,0:T(8,128)(2,1)S(1)} %copy-done.1, bf16[4096,512]{1,0:T(8,128)(2,1)} %all-gather.5.cloned.1.call-done.lall), custom_call_target="tpu_custom_call", output_to_operand_aliasing={{}: (1, {})} | custom-call | flops 1073741824 | bytes 16777216 | tf_op jit(solution)/shard_map/pallas_call | solution.py:138
  (393 shorter events, 231.7 us)
Async XLA Ops:
  7.2 351.0 %all-gather.3.cloned.1.call-start = ((), (), s32[]{:S(2)}) async-start(), calls=%async_computation | async-start | bytes 5242880 | tf_op jit(solution)/shard_map/all_gather | solution.py:207
  7.2 90.1 %collective-permute-start = (bf16[64,4096]{1,0:T(8,128)(2,1)}, bf16[64,4096]{1,0:T(8,128)(2,1)}, u32[]{:S(2)}, u32[]{:S(2)}) collective-permute-start(bf16[64,4096]{1,0:T(8,128)(2,1)} %bitcast.286), channel_id=1, source_target_pairs={{0,4},{4,0},{8,12},{12,8},{16,20},{20,16},{24,28},{28,24},{1,5},{5... | collective-permute-start | bytes 1572872 | tf_op jit(solution)/shard_map/ppermute | solution.py:52
  11.6 20.4 %copy-start.64 = (s32[32]{0:T(128)}, s32[32]{0:T(128)S(1)}, u32[]{:S(2)}) copy-start(s32[32]{0:T(128)S(1)} %get-tuple-element.69) | copy-start | bytes 388
  18.3 79.0 %collective-permute-start.1 = (bf16[1024,512]{0,1:T(8,128)(2,1)}, bf16[1024,512]{0,1:T(8,128)(2,1)}, u32[]{:S(2)}, u32[]{:S(2)}) collective-permute-start(bf16[1024,512]{0,1:T(8,128)(2,1)} %pad_maximum_fusion.3), channel_id=1, source_target_pairs={{0,4},{4,0},{8,12},{12,8},{16,20},{20,16},{24,28},{28,24},{1,5},{5... | collective-permute-start | bytes 3145736 | tf_op jit(solution)/shard_map/ppermute | solution.py:52
  19.5 28.1 %collective-permute-start.2 = (bf16[1024,512]{0,1:T(8,128)(2,1)S(1)}, bf16[1024,512]{0,1:T(8,128)(2,1)S(1)}, u32[]{:S(2)}, u32[]{:S(2)}) collective-permute-start(bf16[1024,512]{0,1:T(8,128)(2,1)S(1)} %copy.137), channel_id=1, source_target_pairs={{0,16},{1,17},{2,18},{3,19}} | collective-permute-start | bytes 3145736 | tf_op jit(solution)/shard_map/ppermute | solution.py:75
  25.7 58.6 %collective-permute-start.5 = (bf16[64,512]{0,1:T(8,128)(2,1)S(1)}, bf16[64,512]{0,1:T(8,128)(2,1)}, u32[]{:S(2)}, u32[]{:S(2)}) collective-permute-start(bf16[64,512]{0,1:T(8,128)(2,1)S(1)} %copy.138), channel_id=1, source_target_pairs={{0,16},{1,17},{2,18},{3,19}} | collective-permute-start | bytes 196616 | tf_op jit(solution)/shard_map/ppermute | solution.py:75
  47.7 23.7 %collective-permute-start.3 = (bf16[1024,512]{0,1:T(8,128)(2,1)S(1)}, bf16[1024,512]{0,1:T(8,128)(2,1)S(1)}, u32[]{:S(2)}, u32[]{:S(2)}) collective-permute-start(bf16[1024,512]{0,1:T(8,128)(2,1)S(1)} %broadcast_select_fusion.4), channel_id=1, source_target_pairs={{0,8},{16,24},{1,9},{17,25},{2,10},{18,26},{3,11},{19,27}} | collective-permute-start | bytes 3145736 | tf_op jit(solution)/shard_map/ppermute | solution.py:75
  59.9 32.7 %copy-start.57 = (pred[4]{0:T(512)(128)(4,1)S(1)}, pred[4]{0:T(512)(128)(4,1)}, u32[]{:S(2)}) copy-start(pred[4]{0:T(512)(128)(4,1)} %get-tuple-element.198) | copy-start | bytes 16
  71.5 25.6 %collective-permute-start.4 = (bf16[1024,512]{0,1:T(8,128)(2,1)S(1)}, bf16[1024,512]{0,1:T(8,128)(2,1)S(1)}, u32[]{:S(2)}, u32[]{:S(2)}) collective-permute-start(bf16[1024,512]{0,1:T(8,128)(2,1)S(1)} %broadcast_select_fusion.5), channel_id=1, source_target_pairs={{0,4},{8,12},{16,20},{24,28},{1,5},{9,13},{17,21},{25,29},{2,6},{1... | collective-permute-start | bytes 3145736 | tf_op jit(solution)/shard_map/ppermute | solution.py:75
  84.3 6.9 collective-permute-start.6
  91.2 5.9 collective-permute-start.7
  100.4 25.7 %collective-permute-start.11 = (bf16[1088,512]{1,0:T(8,128)(2,1)}, bf16[1088,512]{1,0:T(8,128)(2,1)S(1)}, u32[]{:S(2)}, u32[]{:S(2)}) collective-permute-start(bf16[1088,512]{1,0:T(8,128)(2,1)} %copy.88), channel_id=1, source_target_pairs={{0,2},{1,3},{4,6},{5,7},{8,10},{9,11},{12,14},{13,15},{16,18},{17,... | collective-permute-start | bytes 3342344 | tf_op jit(solution)/shard_map/ppermute | solution.py:86
  129.1 12.1 %collective-permute-start.12 = (bf16[1088,512]{1,0:T(8,128)(2,1)}, bf16[1088,512]{1,0:T(8,128)(2,1)}, u32[]{:S(2)}, u32[]{:S(2)}) collective-permute-start(bf16[1088,512]{1,0:T(8,128)(2,1)} %copy.90), channel_id=1, source_target_pairs={{0,1},{1,0},{2,3},{3,2},{4,5},{5,4},{6,7},{7,6},{8,9},{9,8},{10,11... | collective-permute-start | bytes 3342344 | tf_op jit(solution)/shard_map/ppermute | solution.py:52
  131.7 4.0 collective-permute-start.9
  133.1 213.2 %collective-permute-start.8 = (bf16[1024,4096]{1,0:T(8,128)(2,1)}, bf16[1024,4096]{1,0:T(8,128)(2,1)}, u32[]{:S(2)}, u32[]{:S(2)}) collective-permute-start(bf16[1024,4096]{1,0:T(8,128)(2,1)} %bitcast.276), channel_id=1, source_target_pairs={{0,4},{4,0},{8,12},{12,8},{16,20},{20,16},{24,28},{28,24},{1,5},{5... | collective-permute-start | bytes 25165832 | tf_op jit(solution)/shard_map/ppermute | solution.py:52
  137.5 27.3 %collective-permute-start.10 = (f32[512,512]{0,1:T(8,128)S(1)}, f32[512,512]{0,1:T(8,128)}, u32[]{:S(2)}, u32[]{:S(2)}) collective-permute-start(f32[512,512]{0,1:T(8,128)S(1)} %add.456), channel_id=1, source_target_pairs={{0,2},{1,3},{2,0},{3,1},{4,6},{5,7},{6,4},{7,5},{8,10},{9,11},{10,... | collective-permute-start | bytes 3145736 | tf_op jit(solution)/shard_map/ppermute | solution.py:52
  146.6 18.2 %copy-start.29 = (f32[512,512]{0,1:T(8,128)S(1)}, f32[512,512]{0,1:T(8,128)}, u32[]{:S(2)}) copy-start(f32[512,512]{0,1:T(8,128)} %copy-done.28) | copy-start | bytes 3145732
  146.8 17.9 %copy-start.13 = (f32[1024,512]{0,1:T(8,128)}, f32[1024,512]{0,1:T(8,128)S(1)}, u32[]{:S(2)}) copy-start(f32[1024,512]{0,1:T(8,128)S(1)} %slice_convert_fusion) | copy-start | bytes 6291460
  245.3 27.9 %copy-start.32 = (f32[512,128]{0,1:T(8,128)S(1)}, f32[512,128]{0,1:T(8,128)}, u32[]{:S(2)}) copy-start(f32[512,128]{0,1:T(8,128)} %slice.628) | copy-start | bytes 786436
  271.4 27.7 %copy-start.38 = (f32[1024,512]{0,1:T(8,128)S(1)}, f32[1024,512]{0,1:T(8,128)}, u32[]{:S(2)}) copy-start(f32[1024,512]{0,1:T(8,128)} %copy-done.37) | copy-start | bytes 6291460
  273.3 24.9 %copy-start.33 = (f32[512,128]{0,1:T(8,128)}, f32[512,128]{0,1:T(8,128)S(1)}, u32[]{:S(2)}) copy-start(f32[512,128]{0,1:T(8,128)S(1)} %fusion.56) | copy-start | bytes 786436
  273.3 24.8 %collective-permute-start.13 = (f32[512,512]{0,1:T(8,128)S(1)}, f32[512,512]{0,1:T(8,128)S(1)}, u32[]{:S(2)}, u32[]{:S(2)}) collective-permute-start(f32[512,512]{0,1:T(8,128)S(1)} %pad_maximum_fusion.4), channel_id=1, source_target_pairs={{0,2},{1,3},{2,0},{3,1},{4,6},{5,7},{6,4},{7,5},{8,10},{9,11},{10,... | collective-permute-start | bytes 3145736 | tf_op jit(solution)/shard_map/ppermute | solution.py:52
  299.2 31.1 %copy-start.61 = (s32[32]{0:T(128)S(1)}, s32[32]{0:T(128)}, u32[]{:S(2)}) copy-start(s32[32]{0:T(128)} %copy-done.60) | copy-start | bytes 388
  299.2 31.1 %copy-start.63 = (s32[32]{0:T(128)S(1)}, s32[32]{0:T(128)}, u32[]{:S(2)}) copy-start(s32[32]{0:T(128)} %copy-done.62) | copy-start | bytes 388
  299.2 35.2 %copy-start.51 = (bf16[1,64,4096]{2,1,0:T(8,128)(2,1)S(1)}, bf16[1,64,4096]{2,1,0:T(8,128)(2,1)}, u32[]{:S(2)}) copy-start(bf16[1,64,4096]{2,1,0:T(8,128)(2,1)} %param.11) | copy-start | bytes 1572868
  308.8 452.6 %all-gather.5.cloned.1.call-start = ((), (), s32[]{:S(2)}) async-start(), calls=%async_computation.1 | async-start | bytes 5242880 | tf_op jit(solution)/shard_map/all_gather | solution.py:207
  390.5 47.5 %collective-permute-start.15 = (f32[1024,512]{0,1:T(8,128)}, f32[1024,512]{0,1:T(8,128)}, u32[]{:S(2)}, u32[]{:S(2)}) collective-permute-start(f32[1024,512]{0,1:T(8,128)} %pad_maximum_fusion), channel_id=1, source_target_pairs={{0,8},{4,12},{8,0},{12,4},{16,24},{20,28},{24,16},{28,20},{1,9},{5... | collective-permute-start | bytes 6291464 | tf_op jit(solution)/shard_map/ppermute | solution.py:52
  399.5 94.7 %collective-permute-start.22 = (bf16[4096,512]{0,1:T(8,128)(2,1)}, bf16[4096,512]{0,1:T(8,128)(2,1)}, u32[]{:S(2)}, u32[]{:S(2)}) collective-permute-start(bf16[4096,512]{0,1:T(8,128)(2,1)} %copy.115), channel_id=1, source_target_pairs={{0,2},{1,3},{4,6},{5,7},{8,10},{9,11},{12,14},{13,15},{16,18},{17,... | collective-permute-start | bytes 12582920 | tf_op jit(solution)/shard_map/ppermute | solution.py:86
  430.3 23.8 %copy-start.40 = (f32[1024,512]{0,1:T(8,128)}, f32[1024,512]{0,1:T(8,128)S(1)}, u32[]{:S(2)}) copy-start(f32[1024,512]{0,1:T(8,128)S(1)} %get-tuple-element.45) | copy-start | bytes 6291460
  449.1 49.7 %slice-start = ((s8[16777216]{0:T(1024)(128)(4,1)}), s8[4194304]{0:T(1024)(128)(4,1)S(1)}, s32[]{:S(2)}) async-start(s8[16777216]{0:T(1024)(128)(4,1)} %bitcast.273), calls=%async_computation.2 | async-start | bytes 8388608
  454.3 8.1 collective-permute-start.16
  457.1 41.7 %slice-start.1 = ((s8[16777216]{0:T(1024)(128)(4,1)}), s8[4194304]{0:T(1024)(128)(4,1)S(1)}, s32[]{:S(2)}) async-start(s8[16777216]{0:T(1024)(128)(4,1)} %bitcast.273), calls=%async_computation.3 | async-start | bytes 8388608
  461.9 36.9 %slice-start.2 = ((s8[16777216]{0:T(1024)(128)(4,1)}), s8[4194304]{0:T(1024)(128)(4,1)S(1)}, s32[]{:S(2)}) async-start(s8[16777216]{0:T(1024)(128)(4,1)} %bitcast.273), calls=%async_computation.4 | async-start | bytes 8388608
  462.6 36.2 %slice-start.3 = ((s8[16777216]{0:T(1024)(128)(4,1)}), s8[4194304]{0:T(1024)(128)(4,1)S(1)}, s32[]{:S(2)}) async-start(s8[16777216]{0:T(1024)(128)(4,1)} %bitcast.273), calls=%async_computation.5 | async-start | bytes 8388608
  462.6 51.3 %collective-permute-start.17 = (f32[512,512]{0,1:T(8,128)S(1)}, f32[512,512]{0,1:T(8,128)}, u32[]{:S(2)}, u32[]{:S(2)}) collective-permute-start(f32[512,512]{0,1:T(8,128)S(1)} %add.493), channel_id=1, source_target_pairs={{0,2},{1,3},{2,0},{3,1},{4,6},{5,7},{6,4},{7,5},{8,10},{9,11},{10,... | collective-permute-start | bytes 3145736 | tf_op jit(solution)/shard_map/ppermute | solution.py:52
  498.8 162.2 %collective-permute-start.23 = (bf16[4096,512]{0,1:T(8,128)(2,1)}, bf16[4096,512]{0,1:T(8,128)(2,1)}, u32[]{:S(2)}, u32[]{:S(2)}) collective-permute-start(bf16[4096,512]{0,1:T(8,128)(2,1)} %broadcast_select_fusion), channel_id=1, source_target_pairs={{0,1},{1,0},{2,3},{3,2},{4,5},{5,4},{6,7},{7,6},{8,9},{9,8},{10,11... | collective-permute-start | bytes 12582920 | tf_op jit(solution)/shard_map/ppermute | solution.py:52
  502.7 198.9 %collective-permute-start.14 = (f32[256,4096]{1,0:T(8,128)}, f32[256,4096]{1,0:T(8,128)}, u32[]{:S(2)}, u32[]{:S(2)}) collective-permute-start(f32[256,4096]{1,0:T(8,128)} %get-tuple-element.25), channel_id=1, source_target_pairs={{0,8},{4,12},{8,0},{12,4},{16,24},{20,28},{24,16},{28,20},{1,9},{5... | collective-permute-start | bytes 12582920 | tf_op jit(solution)/shard_map/ppermute | solution.py:52
  502.8 200.0 %collective-permute-start.19 = (f32[256,4096]{1,0:T(8,128)}, f32[256,4096]{1,0:T(8,128)}, u32[]{:S(2)}, u32[]{:S(2)}) collective-permute-start(f32[256,4096]{1,0:T(8,128)} %get-tuple-element.24), channel_id=1, source_target_pairs={{0,8},{4,12},{8,0},{12,4},{16,24},{20,28},{24,16},{28,20},{1,9},{5... | collective-permute-start | bytes 12582920 | tf_op jit(solution)/shard_map/ppermute | solution.py:52
  545.1 25.9 %copy-start.17 = (f32[1024,384]{0,1:T(8,128)S(1)}, f32[1024,384]{0,1:T(8,128)}, u32[]{:S(2)}) copy-start(f32[1024,384]{0,1:T(8,128)} %copy-done.16) | copy-start | bytes 4718596
  573.2 25.9 %copy-start.21 = (f32[1024,256]{0,1:T(8,128)S(1)}, f32[1024,256]{0,1:T(8,128)}, u32[]{:S(2)}) copy-start(f32[1024,256]{0,1:T(8,128)} %copy-done.20) | copy-start | bytes 3145732
  599.1 25.7 %copy-start.36 = (f32[1024,128]{0,1:T(8,128)}, f32[1024,128]{0,1:T(8,128)S(1)}, u32[]{:S(2)}) copy-start(f32[1024,128]{0,1:T(8,128)S(1)} %fusion.44) | copy-start | bytes 1572868
  600.6 28.0 %copy-start.25 = (f32[1024,128]{0,1:T(8,128)S(1)}, f32[1024,128]{0,1:T(8,128)}, u32[]{:S(2)}) copy-start(f32[1024,128]{0,1:T(8,128)} %copy-done.24) | copy-start | bytes 1572868
  628.7 23.4 %collective-permute-start.18 = (f32[512,512]{0,1:T(8,128)S(1)}, f32[512,512]{0,1:T(8,128)S(1)}, u32[]{:S(2)}, u32[]{:S(2)}) collective-permute-start(f32[512,512]{0,1:T(8,128)S(1)} %pad_maximum_fusion.5), channel_id=1, source_target_pairs={{0,2},{1,3},{2,0},{3,1},{4,6},{5,7},{6,4},{7,5},{8,10},{9,11},{10,... | collective-permute-start | bytes 3145736 | tf_op jit(solution)/shard_map/ppermute | solution.py:52
  661.0 29.0 %copy-start.52 = (s32[4096]{0:T(1024)S(1)}, s32[4096]{0:T(1024)}, u32[]{:S(2)}) copy-start(s32[4096]{0:T(1024)} %iota_add_fusion) | copy-start | bytes 49156
  701.6 93.8 %collective-permute-start.20 = (f32[256,4096]{1,0:T(8,128)}, f32[256,4096]{1,0:T(8,128)}, u32[]{:S(2)}, u32[]{:S(2)}) collective-permute-start(f32[256,4096]{1,0:T(8,128)} %collective-permute-done.14.oth), channel_id=1, source_target_pairs={{0,4},{4,0},{8,12},{12,8},{16,20},{20,16},{24,28},{28,24},{1,5},{5... | collective-permute-start | bytes 12582920 | tf_op jit(solution)/shard_map/ppermute | solution.py:52
  702.8 178.4 %collective-permute-start.21 = (f32[256,4096]{1,0:T(8,128)}, f32[256,4096]{1,0:T(8,128)}, u32[]{:S(2)}, u32[]{:S(2)}) collective-permute-start(f32[256,4096]{1,0:T(8,128)} %collective-permute-done.19.oth), channel_id=1, source_target_pairs={{0,4},{4,0},{8,12},{12,8},{16,20},{20,16},{24,28},{28,24},{1,5},{5... | collective-permute-start | bytes 12582920 | tf_op jit(solution)/shard_map/ppermute | solution.py:52
  705.5 33.4 %copy-start.53 = (s32[4096]{0:T(1024)S(1)}, s32[4096]{0:T(1024)}, u32[]{:S(2)}) copy-start(s32[4096]{0:T(1024)} %broadcast_add_fusion) | copy-start | bytes 49156
  744.4 17.0 %copy-start.1 = (bf16[1024,512]{1,0:T(8,128)(2,1)S(1)}, bf16[1024,512]{1,0:T(8,128)(2,1)}, u32[]{:S(2)}) copy-start(bf16[1024,512]{1,0:T(8,128)(2,1)} %fusion.31.lrow) | copy-start | bytes 3145732
  (52 other events, 277.8 us)
Sparse Core Ops, SparseCore 0:
  309.0 34.3 all-gather.2
  661.1 32.5 all-gather.4
